TPU v7x, 256 devices: a whole 4x4x8 slice. The times are simulated.
256 devices in a mesh: segment: 2 (over core), rows: 32 (over z, x), dp: 4 (over y).
Axes of the slice: x: 4, y: 4, z: 8, core: 2. Of those that a mesh axis runs over, the one named last changes fastest.
Arguments:
- coarse: bfloat16 [8, 100, 384, 256], P(('segment', 'dp'), None, 'rows'), may hold values from -6 to 6
- target: bfloat16 [8, 64, 384, 256], P(('segment', 'dp'), None, 'rows'), may hold values from -6 to 6
- noise: bfloat16 [8, 32, 64, 64, 144], P(('segment', 'dp'), 'rows'), may hold values from -6 to 6
- regions: int32 [8, 32, 32, 4], P(('segment', 'dp')), may hold values from 0 to 244, as said below
- reg_conv: bfloat16 [128, 900], replicated, may hold values from -0.1875 to 0.1875
- reg_out: bfloat16 [64, 128], replicated, may hold values from -0.5 to 0.5
- conv_one: bfloat16 [128, 1152], replicated, may hold values from -0.1875 to 0.1875
- conv_two: bfloat16 [128, 1152], replicated, may hold values from -0.1875 to 0.1875
- out_proj: bfloat16 [64, 128], replicated, may hold values from -0.5 to 0.5
- step_embed: float32 [32, 128], replicated, may hold values from -3 to 3
Outputs:
- mean_field: bfloat16 [8, 64, 384, 256], P(('segment', 'dp'), None, 'rows')
- owner_loss: float32 [8, 32], P(('segment', 'dp'), 'rows')
- grad_conv_one: float32 [128, 1152], replicated
- grad_conv_two: float32 [128, 1152], replicated
- grad_out_proj: float32 [64, 128], replicated
- grad_embed: float32 [32, 128], replicated
Inputs may be any that keep to these rules, and one draw needn't show every extreme that they name: `regions`: for sample s, strip i and entry k: entry 0 is the patch's row offset within strip i (0 on the last strip), entry 1 its first column, at most 244, entry 2 its owner, entry 3 its noise level below 32. Every owner receives 2 * 32, 32 or 16 patches of a sample; for each owner with 64 there is one with 32 and two with 16. No strip lists more than 2 patches for one owner, and some strip lists exactly 2 for one owner.
All inputs are finite; a program needn't handle non-finite values.
Results may differ from a plain program's by a relative error of at most 0.0048.
Values may be sent and summed in bfloat16 or wider, within the bound.
A program may use at most 192 MiB of HBM per device.

v0:
```python
import math

import jax
import jax.numpy as jnp
from jax import lax
from jax.experimental import pallas as pl
from jax.experimental.pallas import tpu as pltpu
from jax.sharding import PartitionSpec as P

PATCH = 12


TAPS = ((-1, -1), (-1, 0), (-1, 1), (0, -1), (0, 0), (0, 1), (1, -1), (1, 0), (1, 1))


def padded_2(cells, sides, width):
    for axis, dim in sides:
        count = lax.axis_size(axis)
        ends = count - 1
        head = lax.slice_in_dim(cells, 0, width, axis=dim)
        tail = lax.slice_in_dim(cells, cells.shape[dim] - width, cells.shape[dim], axis=dim)
        cells = jnp.concatenate(
            [
                lax.ppermute(tail, axis, [(i, (i + 1) % count) for i in range(ends)]),
                cells,
                lax.ppermute(head, axis, [((i + 1) % count, i) for i in range(ends)]),
            ],
            axis=dim,
        )
    return cells


def shifted_2(block, axis, distance):
    devices = range(lax.axis_size(axis))
    route = [(i - distance, i) for i in devices if i - distance in devices]
    return lax.ppermute(block, axis, route)


def shifted(values, row_step, col_step, stride):
    length = values.shape[-1]
    margin = stride + 1
    widths = [(0, 0)] * (values.ndim - 1) + [(margin, margin)]
    padded = jnp.pad(values, widths)
    offset = margin + row_step * stride + col_step
    moved = lax.slice_in_dim(padded, offset, offset + length, axis=values.ndim - 1)
    column = jnp.arange(length, dtype=jnp.int32) % stride + col_step
    inside = (column >= 0) & (column < stride)
    return jnp.where(inside, moved, jnp.zeros((), moved.dtype))


def columns(values, stride):
    return jnp.concatenate(
        [shifted(values, row_step, col_step, stride) for row_step, col_step in TAPS], axis=-2
    )


def fold(gradients, stride):
    width = gradients.shape[-2] // 9
    result = jnp.zeros(gradients.shape[:-2] + (width, gradients.shape[-1]), jnp.float32)
    for position, (row_step, col_step) in enumerate(TAPS):
        piece = gradients[..., position * width : (position + 1) * width, :]
        result = result + shifted(piece, -row_step, -col_step, stride)
    return result


def noise_levels(level_count):
    steps_f = jnp.arange(level_count, dtype=jnp.float32)
    return 0.1 * jnp.exp(steps_f * (math.log(100.0) / (level_count - 1)))


def silu_slope(values):
    gate = jax.nn.sigmoid(values)
    return gate * (1.0 + values * (1.0 - gate))


def product(form, left, right):
    return jnp.einsum(form, left, right, preferred_element_type=jnp.float32)


def regress(grid_rows, reg_conv, reg_out):
    channels, height, width = grid_rows.shape
    hidden_count = reg_conv.shape[0]
    kernel = reg_conv.reshape(hidden_count, 3, 3, channels).transpose(1, 2, 3, 0)
    hidden = lax.conv_general_dilated(
        grid_rows[None],
        kernel,
        window_strides=(1, 1),
        padding=((0, 0), (1, 1)),
        dimension_numbers=("NCHW", "HWIO", "NHWC"),
        preferred_element_type=jnp.float32,
    )[0]
    activated = jax.nn.silu(hidden).astype(jnp.bfloat16)
    return product("rqo,co->rqc", activated, reg_out).astype(jnp.bfloat16)


def patch_block(mean_part, target_part, noise_part, step_ids, in_use, weights):
    conv_one, conv_two, out_proj, step_embed = weights
    stride = PATCH
    level_count = step_embed.shape[0]
    sigma_table = noise_levels(level_count)
    step_hot = (step_ids[:, None] == jnp.arange(level_count, dtype=jnp.int32)[None, :]).astype(
        jnp.float32
    )
    sigma = jnp.sum(step_hot * sigma_table[None, :], axis=1)
    sigma_sq = sigma * sigma + 1.0
    scale_in = (1.0 / jnp.sqrt(sigma_sq))[:, None, None]
    scale_skip = (1.0 / sigma_sq)[:, None, None]
    scale_out = (sigma / jnp.sqrt(sigma_sq))[:, None, None]
    weight_loss = sigma_sq / (sigma * sigma)
    mean_float = mean_part.astype(jnp.float32)
    residual = target_part.astype(jnp.float32) - mean_float
    noisy = residual + sigma[:, None, None] * noise_part.astype(jnp.float32)
    inputs = jnp.concatenate([scale_in * noisy, mean_float], axis=1).astype(jnp.bfloat16)
    cols_in = columns(inputs, stride)
    embedded = jnp.sum(step_hot[:, :, None] * step_embed[None, :, :], axis=1)
    pre_one = product("ok,bkp->bop", conv_one, cols_in) + embedded[:, :, None]
    act_one = jax.nn.silu(pre_one).astype(jnp.bfloat16)
    cols_one = columns(act_one, stride)
    pre_two = product("ok,bkp->bop", conv_two, cols_one)
    act_two = jax.nn.silu(pre_two).astype(jnp.bfloat16)
    output = product("co,bop->bcp", out_proj, act_two)
    error = scale_skip * noisy + scale_out * output - residual
    losses = weight_loss * jnp.mean(error * error, axis=(1, 2)) * in_use
    factor = 2.0 * weight_loss * in_use / (error.shape[1] * error.shape[2])
    grad_output = (factor[:, None, None] * scale_out * error).astype(jnp.bfloat16)
    grad_proj = product("bcp,bop->co", grad_output, act_two)
    grad_act_two = product("co,bcp->bop", out_proj, grad_output)
    grad_pre_two = (grad_act_two * silu_slope(pre_two)).astype(jnp.bfloat16)
    grad_two = product("bop,bkp->ok", grad_pre_two, cols_one)
    grad_cols = product("ok,bop->bkp", conv_two, grad_pre_two)
    grad_act_one = fold(grad_cols, stride)
    grad_pre_one = (grad_act_one * silu_slope(pre_one)).astype(jnp.bfloat16)
    grad_one = product("bop,bkp->ok", grad_pre_one, cols_in)
    pixel_sums = jnp.sum(grad_pre_one, axis=2, dtype=jnp.float32)
    grad_table = jnp.sum(step_hot[:, :, None] * pixel_sums[:, None, :], axis=0)
    return (losses, (grad_one, grad_two, grad_proj, grad_table))


def run_blocks(mean_part, target_part, noise_part, step_ids, in_use, weights):
    patch_count = mean_part.shape[0]
    blocks = patch_count // 4

    def regroup(values):
        return values.reshape((blocks, 4) + values.shape[1:])

    def advance(running, group_block):
        losses, gradients = patch_block(
            group_block[0], group_block[1], group_block[2], group_block[3], group_block[4], weights
        )
        summed = (
            running[0] + gradients[0],
            running[1] + gradients[1],
            running[2] + gradients[2],
            running[3] + gradients[3],
        )
        return (summed, losses)

    initial = (
        jnp.zeros(weights[0].shape, jnp.float32),
        jnp.zeros(weights[1].shape, jnp.float32),
        jnp.zeros(weights[2].shape, jnp.float32),
        jnp.zeros(weights[3].shape, jnp.float32),
    )
    stacked = (
        regroup(mean_part),
        regroup(target_part),
        regroup(noise_part),
        regroup(step_ids),
        regroup(in_use),
    )
    gradients, losses = lax.scan(advance, initial, stacked)
    return (losses.reshape(patch_count), gradients)


def tap_masks(rows):
    cell = jnp.arange(rows, dtype=jnp.int32) % (PATCH * PATCH)
    line = cell // PATCH
    place = cell % PATCH
    cols = []
    for row_step, col_step in TAPS:
        inside = (line + row_step >= 0) & (line + row_step < PATCH)
        inside = inside & (place + col_step >= 0) & (place + col_step < PATCH)
        cols.append(inside.astype(jnp.float32))
    cols += [jnp.zeros((rows,), jnp.float32)] * (16 - len(cols))
    return jnp.stack(cols, axis=1)


def sig(values):
    return 1.0 / (1.0 + jnp.exp(-values))


def patch_kernel(xin_ref, skip_ref, scale_ref, emb_ref, mask_ref, w1t_ref, w2t_ref, w2_ref,
                 pt_ref, pm_ref, err_ref, sums_ref, g1_ref, g2_ref, gp_ref, cin_ref, cone_ref):
    rows = xin_ref.shape[0]
    groups = sums_ref.shape[0]
    cells = rows // groups
    channels = xin_ref.shape[1]

    @pl.when(pl.program_id(0) == 0)
    def _():
        g1_ref[...] = jnp.zeros_like(g1_ref)
        g2_ref[...] = jnp.zeros_like(g2_ref)
        gp_ref[...] = jnp.zeros_like(gp_ref)

    def stack(values, target):
        for tap, (row_step, col_step) in enumerate(TAPS):
            shift = row_step * PATCH + col_step
            moved = values if shift == 0 else pltpu.roll(values, (-shift) % rows, 0)
            moved = moved * mask_ref[:, tap : tap + 1]
            target[:, tap * channels : (tap + 1) * channels] = moved.astype(target.dtype)

    stack(xin_ref[...].astype(jnp.float32), cin_ref)
    pre_one = jnp.dot(cin_ref[...], w1t_ref[...], preferred_element_type=jnp.float32)
    pre_one = pre_one + emb_ref[...]
    gate_one = sig(pre_one)
    act_one = (pre_one * gate_one).astype(jnp.bfloat16)
    stack(act_one.astype(jnp.float32), cone_ref)
    pre_two = jnp.dot(cone_ref[...], w2t_ref[...], preferred_element_type=jnp.float32)
    gate_two = sig(pre_two)
    act_two = (pre_two * gate_two).astype(jnp.bfloat16)
    output = jnp.dot(act_two, pt_ref[...], preferred_element_type=jnp.float32)
    error = skip_ref[...] + scale_ref[:, 0:1] * output
    err_ref[...] = error
    grad_output = (scale_ref[:, 1:2] * error).astype(jnp.bfloat16)
    contract = (((0,), (0,)), ((), ()))
    gp_ref[...] += lax.dot_general(grad_output, act_two, contract, preferred_element_type=jnp.float32)
    grad_act_two = jnp.dot(grad_output, pm_ref[...], preferred_element_type=jnp.float32)
    slope_two = gate_two * (1.0 + pre_two * (1.0 - gate_two))
    grad_pre_two = (grad_act_two * slope_two).astype(jnp.bfloat16)
    g2_ref[...] += lax.dot_general(grad_pre_two, cone_ref[...], contract, preferred_element_type=jnp.float32)
    grad_act_one = jnp.zeros((rows, channels), jnp.float32)
    for tap, (row_step, col_step) in enumerate(TAPS):
        shift = row_step * PATCH + col_step
        piece = jnp.dot(grad_pre_two, w2_ref[:, tap * channels : (tap + 1) * channels],
                        preferred_element_type=jnp.float32)
        moved = piece if shift == 0 else pltpu.roll(piece, shift % rows, 0)
        grad_act_one = grad_act_one + moved * mask_ref[:, 8 - tap : 9 - tap]
    slope_one = gate_one * (1.0 + pre_one * (1.0 - gate_one))
    grad_pre_one = (grad_act_one * slope_one).astype(jnp.bfloat16)
    g1_ref[...] += lax.dot_general(grad_pre_one, cin_ref[...], contract, preferred_element_type=jnp.float32)
    wide = grad_pre_one.astype(jnp.float32)
    for group in range(groups):
        sums_ref[group : group + 1, :] = jnp.sum(wide[group * cells : (group + 1) * cells], axis=0, keepdims=True)


def patch_pass(xin, skip, scale, emb, conv_one, conv_two, out_proj, group=8, interpret=False):
    rows_all, channels = xin.shape
    cells = PATCH * PATCH
    patches = rows_all // cells
    rows = group * cells
    steps = patches // group
    width = conv_one.shape[1]
    outs = conv_one.shape[0]
    targets = out_proj.shape[0]
    masks = tap_masks(rows)
    block = lambda shape: pl.BlockSpec(shape, lambda i: (i, 0))
    whole = lambda shape: pl.BlockSpec(shape, lambda i: (0, 0))
    return pl.pallas_call(
        patch_kernel,
        grid=(steps,),
        in_specs=[
            block((rows, channels)),
            block((rows, targets)),
            block((rows, 8)),
            block((rows, outs)),
            whole((rows, 16)),
            whole((width, outs)),
            whole((width, outs)),
            whole((outs, width)),
            whole((outs, targets)),
            whole((targets, outs)),
        ],
        out_specs=[
            block((rows, targets)),
            block((group, outs)),
            whole((outs, width)),
            whole((outs, width)),
            whole((targets, outs)),
        ],
        out_shape=[
            jax.ShapeDtypeStruct((rows_all, targets), jnp.float32),
            jax.ShapeDtypeStruct((patches, outs), jnp.float32),
            jax.ShapeDtypeStruct((outs, width), jnp.float32),
            jax.ShapeDtypeStruct((outs, width), jnp.float32),
            jax.ShapeDtypeStruct((targets, outs), jnp.float32),
        ],
        scratch_shapes=[pltpu.VMEM((rows, width), jnp.bfloat16), pltpu.VMEM((rows, width), jnp.bfloat16)],
        compiler_params=pltpu.CompilerParams(dimension_semantics=("arbitrary",)),
        interpret=interpret,
    )(xin, skip, scale, emb, masks, conv_one.T, conv_two.T, conv_two, out_proj.T, out_proj)


def kernel_blocks(mean_part, target_part, noise_part, step_ids, in_use, weights, interpret=False):
    conv_one, conv_two, out_proj, step_embed = weights
    patch_count, targets, cells = mean_part.shape
    level_count = step_embed.shape[0]
    sigma_table = noise_levels(level_count)
    step_hot = (step_ids[:, None] == jnp.arange(level_count, dtype=jnp.int32)[None, :]).astype(
        jnp.float32
    )
    sigma = jnp.sum(step_hot * sigma_table[None, :], axis=1)
    sigma_sq = sigma * sigma + 1.0
    scale_in = (1.0 / jnp.sqrt(sigma_sq))[:, None, None]
    scale_skip = (1.0 / sigma_sq)[:, None, None]
    scale_out = sigma / jnp.sqrt(sigma_sq)
    weight_loss = sigma_sq / (sigma * sigma)
    mean_float = mean_part.astype(jnp.float32)
    residual = target_part.astype(jnp.float32) - mean_float
    noisy = residual + sigma[:, None, None] * noise_part.astype(jnp.float32)
    inputs = jnp.concatenate([scale_in * noisy, mean_float], axis=1).astype(jnp.bfloat16)
    xin = jnp.swapaxes(inputs, 1, 2).reshape(patch_count * cells, 2 * targets)
    skip = jnp.swapaxes(scale_skip * noisy - residual, 1, 2).reshape(patch_count * cells, targets)
    factor = 2.0 * weight_loss * in_use / (targets * cells)
    per_patch = jnp.stack([scale_out, factor * scale_out], axis=1)
    per_patch = jnp.pad(per_patch, ((0, 0), (0, 6)))
    scale = jnp.broadcast_to(per_patch[:, None, :], (patch_count, cells, 8)).reshape(-1, 8)
    embedded = jnp.sum(step_hot[:, :, None] * step_embed[None, :, :], axis=1)
    emb = jnp.broadcast_to(embedded[:, None, :], (patch_count, cells, embedded.shape[1]))
    emb = emb.reshape(patch_count * cells, embedded.shape[1])
    error, pixel_sums, grad_one, grad_two, grad_proj = patch_pass(
        xin, skip, scale, emb, conv_one, conv_two, out_proj, interpret=interpret
    )
    error = error.reshape(patch_count, cells * targets)
    losses = weight_loss * jnp.mean(error * error, axis=1) * in_use
    grad_table = jnp.sum(step_hot[:, :, None] * pixel_sums[:, None, :], axis=0)
    return (losses, (grad_one, grad_two, grad_proj, grad_table))


def owner_tables(region_rows, strip_index):
    owners = region_rows[:, :, 2]
    earlier = (
        jnp.arange(owners.shape[1], dtype=jnp.int32)[None, :, None]
        > jnp.arange(owners.shape[1], dtype=jnp.int32)[None, None, :]
    )
    same = owners[:, :, None] == owners[:, None, :]
    pair_rank = jnp.sum((same & earlier).astype(jnp.int32), axis=2)
    mine = (owners == strip_index).astype(jnp.int32)
    flat = mine.reshape(-1)
    owner_slot = (jnp.cumsum(flat) - flat).reshape(owners.shape)
    return (owners, pair_rank, owner_slot)


def noise_routes(region_rows, owners, pair_rank, owner_slot, strip_index, capacity):
    hits = (
        (owners == strip_index)[:, :, None]
        & (pair_rank[:, :, None] == jnp.arange(capacity, dtype=jnp.int32)[None, None, :])
    ).astype(jnp.int32)
    return jnp.sum(hits * owner_slot[:, :, None], axis=1)


def exchange_sum(flat, steps):
    spread = 1
    for _, distance in steps:
        spread *= 2
    size = flat.shape[0]
    unit = spread * 8
    padded = (size + unit - 1) // unit * unit
    values = jnp.pad(flat, (0, padded - size))
    places = {axis: lax.axis_index(axis) for axis, _ in steps}
    for axis, distance in steps:
        count = lax.axis_size(axis)
        half = values.shape[0] // 2
        low, high = values[:half], values[half:]
        upper = (places[axis] // distance) % 2 == 1
        route = [(i, i ^ distance) for i in range(count)]
        kept = jnp.where(upper, high, low)
        sent = jnp.where(upper, low, high)
        values = kept + lax.ppermute(sent, axis, route)
    for axis, distance in reversed(steps):
        count = lax.axis_size(axis)
        upper = (places[axis] // distance) % 2 == 1
        route = [(i, i ^ distance) for i in range(count)]
        other = lax.ppermute(values, axis, route)
        values = jnp.where(
            upper, jnp.concatenate([other, values]), jnp.concatenate([values, other])
        )
    return values[:size]


def reduce_steps():
    sizes = {axis: lax.axis_size(axis) for axis in ("segment", "rows", "dp")}
    steps = []
    distance = 1
    while distance < max(sizes.values()):
        for axis in ("segment", "rows", "dp"):
            if distance < sizes[axis]:
                steps.append((axis, distance))
        distance *= 2
    return steps


def cut_patches(source_grid, row_at, col_at, height):
    zero_index = jnp.zeros((), jnp.int32)

    def cut(row_start, col_start):
        piece = lax.dynamic_slice(
            source_grid,
            (zero_index, zero_index, row_start, col_start),
            (2, source_grid.shape[1], height, height),
        )
        return piece.reshape(2, source_grid.shape[1], height * height)

    return jax.vmap(cut)(row_at, col_at)


def per_device(
    coarse, target, noise, regions, reg_conv, reg_out, conv_one, conv_two, out_proj, step_embed
):
    strips = lax.axis_size("rows")
    strip_index = lax.axis_index("rows")
    sample_count = lax.axis_size("segment") * lax.axis_size("dp")
    sample_index = lax.axis_index("segment") * lax.axis_size("dp") + lax.axis_index("dp")
    region_rows = regions[0]
    per_strip = region_rows.shape[1]
    capacity = max(2, (2 * per_strip + strips - 1) // strips)
    weights = (conv_one, conv_two, out_proj, step_embed)
    owners, pair_rank, owner_slot = owner_tables(region_rows, strip_index)
    send_slot = noise_routes(region_rows, owners, pair_rank, owner_slot, strip_index, capacity)
    outgoing = jnp.take(noise[0, 0], send_slot.reshape(-1), axis=0)
    outgoing = outgoing.reshape((strips, capacity) + outgoing.shape[1:])
    received = lax.all_to_all(outgoing, "rows", split_axis=0, concat_axis=0, tiled=True)
    count = strips
    above = lax.ppermute(coarse[:, :, -1:], "rows", [(i, i + 1) for i in range(count - 1)])
    after = lax.ppermute(coarse, "rows", [(i + 1, i) for i in range(count - 1)])
    height = coarse.shape[2]
    later = lax.ppermute(target[:, :, : height - 1], "rows", [(i + 1, i) for i in range(count - 1)])
    rimmed = jnp.concatenate([above, coarse, after], axis=2)
    mean_all = jnp.transpose(regress(rimmed[0], reg_conv, reg_out), (2, 0, 1))
    mean_strip = mean_all[:, :height]
    own_regions = lax.dynamic_index_in_dim(region_rows, strip_index, 0, keepdims=False)
    own_pairs = lax.dynamic_index_in_dim(pair_rank, strip_index, 0, keepdims=False)
    extended = jnp.stack([mean_all[:, : 2 * height - 1], jnp.concatenate([target[0], later[0]], axis=1)])
    patches = cut_patches(extended, own_regions[:, 0], own_regions[:, 1], height)
    flat_recv = received.reshape((strips * capacity,) + received.shape[2:])
    patch_noise = jnp.take(flat_recv, own_regions[:, 2] * capacity + own_pairs, axis=0)
    in_use = jnp.ones((per_strip,), jnp.float32)
    losses, gradients = kernel_blocks(
        patches[:, 0], patches[:, 1], patch_noise, own_regions[:, 3], in_use, weights
    )
    owner_hot = (own_regions[:, 2][:, None] == jnp.arange(strips, dtype=jnp.int32)[None, :])
    owner_part = jnp.sum(owner_hot.astype(jnp.float32) * losses[:, None], axis=0)
    sample_hot = (jnp.arange(sample_count, dtype=jnp.int32) == sample_index).astype(jnp.float32)
    owner_table = sample_hot[:, None] * owner_part[None, :]
    pieces = (gradients[0], gradients[1], gradients[2], gradients[3], owner_table)
    flat = jnp.concatenate([piece.reshape(-1) for piece in pieces])
    summed = exchange_sum(flat, reduce_steps())
    results = []
    offset = 0
    for piece in pieces:
        results.append(summed[offset : offset + piece.size].reshape(piece.shape))
        offset += piece.size
    table = results[4]
    owner_total = lax.dynamic_slice(table, (sample_index, strip_index), (1, 1))
    return (mean_strip[None], owner_total, results[0], results[1], results[2], results[3])


def solution(mesh):
    placed = (
        P(("segment", "dp"), None, "rows", None),
        P(("segment", "dp"), None, "rows", None),
        P(("segment", "dp"), "rows", None, None, None),
        P(("segment", "dp"), None, None, None),
        P(),
        P(),
        P(),
        P(),
        P(),
        P(),
    )
    return jax.shard_map(
        per_device,
        mesh=mesh,
        in_specs=placed,
        out_specs=(
            P(("segment", "dp"), None, "rows", None),
            P(("segment", "dp"), "rows"),
            P(),
            P(),
            P(),
            P(),
        ),
        check_vma=False,
    )
```

profile of v0, /device:TPU:1, one launch (start us, length us, event | category | flops | bytes accessed | tf_op | source)
XLA Modules:
  0.0 255.0 jit_solution(8412695923624328732)
XLA Ops:
  3.5 5.2 %collective-permute-start = (bf16[1,100,1,256]{3,1,2,0:T(8,128)(2,1)}, bf16[1,100,1,256]{3,1,2,0:T(8,128)(2,1)}, u32[]{:S(2)}, u32[]{:S(2)}) collective-permute-start(bf16[1,100,1,256]{3,1,2,0:T(8,128)(2,1)} %slice.112), channel_id=1, source_target_pairs={{0,4},{4,8},{8,12},{12,16},{16,20},{20,24},{24,28},{28,32},{32,36}... | collective-permute-start | bytes 153608 | tf_op jit(solution)/shard_map/ppermute | solution.py:423
  14.7 2.0 gather_fusion.1
  16.7 3.2 %broadcast_select_fusion = bf16[32,2,64,144]{3,2,1,0:T(8,128)(2,1)} fusion(bf16[32,2,64,144]{3,2,1,0:T(8,128)(2,1)} %bitcast.93, pred[32,2]{1,0:T(8,128)(4,1)S(1)} %copy.68), kind=kLoop, calls=%fused_computation.10 | loop fusion | flops 589824 | bytes 2359360 | tf_op jit(solution)/shard_map/jit(_take)/select_n | solution.py:419
  19.9 14.4 %all-to-all-start = ((bf16[32,2,64,144]{3,2,1,0:T(8,128)(2,1)}), bf16[32,2,64,144]{3,2,1,0:T(8,128)(2,1)}, u32[]{:S(2)}, u32[]{:S(2)}) async-start(bf16[32,2,64,144]{3,2,1,0:T(8,128)(2,1)} %broadcast_select_fusion), calls=%async_computation | async-start | bytes 4194304 | tf_op jit(solution)/shard_map/all_to_all | solution.py:421
  45.8 5.4 %copy.63 = bf16[1,100,25,256]{1,0,3,2:T(2,128)(2,1)} copy(bf16[1,100,25,256]{3,1,2,0:T(8,128)(2,1)S(1)} %pad_maximum_fusion.1) | data formatting | bytes 2560000 | tf_op jit(solution)/shard_map/concatenate | solution.py:427
  51.3 15.6 %fusion.20 = f32[1,23,256,128]{3,0,2,1:T(1,128)S(1)} fusion(bf16[1,100,25,256]{1,0,3,2:T(2,128)(2,1)} %copy.63, bf16[128,3,3,100]{0,3,2,1:T(8,128)(2,1)S(1)} %copy-done.13), kind=kOutput, calls=%fused_computation.136 | convolution fusion | flops 1353062400 | bytes 4525056 | tf_op jit(solution)/shard_map/conv_general_dilated | solution.py:84
  69.0 5.5 %copy.64 = bf16[2,64,23,256]{1,0,3,2:T(2,128)(2,1)} copy(bf16[2,64,23,256]{3,1,2,0:T(8,128)(2,1)S(1)} %pad_maximum_fusion) | data formatting | bytes 3014656 | tf_op jit(solution)/shard_map/stack | solution.py:432
  74.5 8.6 %gather_fusion = bf16[32,2,64,12,12]{2,1,4,3,0:T(2,128)(2,1)S(1)} fusion(bf16[2,64,23,256]{1,0,3,2:T(2,128)(2,1)} %copy.64, s32[32]{0:T(128)S(1)} %get-tuple-element.43), kind=kCustom, calls=%fused_computation | custom fusion | bytes 2359808 | tf_op jit(solution)/shard_map/vmap()/gather | solution.py:396
  83.2 5.4 %fusion.18 = (bf16[32,1,64,144]{2,1,3,0:T(2,128)(2,1)}, bf16[32,1,64,144]{2,1,3,0:T(2,128)(2,1)}) fusion(bf16[32,2,64,144]{2,1,3,0:T(2,128)(2,1)S(1)} %bitcast.88), kind=kLoop, calls=%fused_computation.134 | loop fusion | bytes 2359296 | tf_op jit(solution)/shard_map/slice | solution.py:438
  88.6 4.8 %copy.89 = bf16[32,1,64,144]{3,2,0,1:T(8,128)(2,1)S(1)} copy(bf16[32,1,64,144]{2,1,3,0:T(2,128)(2,1)} %get-tuple-element.35) | data formatting | bytes 1179648
  93.4 3.4 %copy.88 = bf16[32,1,64,144]{3,2,0,1:T(8,128)(2,1)} copy(bf16[32,1,64,144]{2,1,3,0:T(2,128)(2,1)S(1)} %copy-done.2) | data formatting | bytes 1179648
  96.9 3.2 %gather_fusion.2 = bf16[32,64,144]{2,1,0:T(8,128)(2,1)} fusion(bf16[64,64,144]{2,1,0:T(8,128)(2,1)} %bitcast.23, s32[1024]{0:T(1024)S(1)} %pad_clamp_fusion), kind=kCustom, calls=%fused_computation.2 | custom fusion | bytes 1179776 | tf_op jit(solution)/shard_map/jit(_take)/gather | solution.py:435
  100.0 2.4 subtract_bitcast_fusion
  104.2 3.8 %copy.70 = bf16[32,144,128]{2,1,0:T(8,128)(2,1)} copy(bf16[32,144,128]{1,2,0:T(8,128)(2,1)} %maximum_bitcast_fusion) | data formatting | bytes 2359296 | tf_op jit(solution)/shard_map/transpose | solution.py:311
  108.0 2.1 copy.71
  113.4 29.0 %shard_map.145 = (f32[4608,64]{1,0:T(8,128)}, f32[32,128]{1,0:T(8,128)}, f32[128,1152]{1,0:T(8,128)}, f32[128,1152]{1,0:T(8,128)}, f32[64,128]{1,0:T(8,128)}) custom-call(bf16[4608,128]{1,0:T(8,128)(2,1)} %bitcast.95, f32[4608,64]{1,0:T(8,128)} %bitcast.89, f32[4608,8]{1,0:T(8,128)} %bitcast.90, f32[4608,128]{1,0:T(8,128)} %bitcast.91, ...), custom_call_target="tpu_custom_call" | custom-call | tf_op jit(solution)/shard_map/pallas_call | solution.py:258
  144.0 2.3 multiply_reduce_fusion
  153.4 7.1 %collective-permute-done.4 = f32[77312]{0:T(1024)S(1)} collective-permute-done((f32[77312]{0:T(1024)S(1)}, f32[77312]{0:T(1024)S(1)}, u32[]{:S(2)}, u32[]{:S(2)}) %collective-permute-start.4) | collective-permute-done | bytes 309280 | tf_op jit(solution)/shard_map/ppermute | solution.py:368
  162.0 2.8 %collective-permute-done.5 = f32[38656]{0:T(1024)S(1)} collective-permute-done((f32[38656]{0:T(1024)S(1)}, f32[38656]{0:T(1024)S(1)}, u32[]{:S(2)}, u32[]{:S(2)}) %collective-permute-start.5) | collective-permute-done | bytes 154656 | tf_op jit(solution)/shard_map/ppermute | solution.py:368
  164.8 3.0 %collective-permute-start.6 = (f32[19328]{0:T(1024)S(1)}, f32[19328]{0:T(1024)S(1)}, u32[]{:S(2)}, u32[]{:S(2)}) collective-permute-start(f32[19328]{0:T(1024)S(1)} %slice_select_fusion.2), channel_id=1, source_target_pairs={{0,8},{4,12},{8,0},{12,4},{16,24},{20,28},{24,16},{28,20},{32,40},... | collective-permute-start | bytes 231944 | tf_op jit(solution)/shard_map/ppermute | solution.py:368
  169.7 3.0 %collective-permute-start.7 = (f32[9664]{0:T(1024)S(1)}, f32[9664]{0:T(1024)S(1)}, u32[]{:S(2)}, u32[]{:S(2)}) collective-permute-start(f32[9664]{0:T(1024)S(1)} %slice_select_fusion.3), channel_id=1, source_target_pairs={{0,2},{1,3},{2,0},{3,1},{4,6},{5,7},{6,4},{7,5},{8,10},{9,11},{10,... | collective-permute-start | bytes 115976 | tf_op jit(solution)/shard_map/ppermute | solution.py:368
  177.2 2.4 collective-permute-start.9
  180.8 5.7 %collective-permute-start.10 = (f32[1208]{0:T(1024)S(1)}, f32[1208]{0:T(1024)S(1)}, u32[]{:S(2)}, u32[]{:S(2)}) collective-permute-start(f32[1208]{0:T(1024)S(1)} %slice_select_fusion.6), channel_id=1, source_target_pairs={{0,64},{4,68},{8,72},{12,76},{16,80},{20,84},{24,88},{28,92},{32,9... | collective-permute-start | bytes 14504 | tf_op jit(solution)/shard_map/ppermute | solution.py:368
  187.6 5.4 %collective-permute-start.11 = (f32[1208]{0:T(1024)S(1)}, f32[1208]{0:T(1024)S(1)}, u32[]{:S(2)}, u32[]{:S(2)}) collective-permute-start(f32[1208]{0:T(1024)S(1)} %select_add_fusion.7), channel_id=1, source_target_pairs={{0,64},{4,68},{8,72},{12,76},{16,80},{20,84},{24,88},{28,92},{32,9... | collective-permute-start | bytes 14504 | tf_op jit(solution)/shard_map/ppermute | solution.py:373
  194.2 2.3 collective-permute-start.12
  200.5 2.9 %collective-permute-start.14 = (f32[9664]{0:T(1024)S(1)}, f32[9664]{0:T(1024)S(1)}, u32[]{:S(2)}, u32[]{:S(2)}) collective-permute-start(f32[9664]{0:T(1024)S(1)} %maximum_select_fusion.12), channel_id=1, source_target_pairs={{0,2},{1,3},{2,0},{3,1},{4,6},{5,7},{6,4},{7,5},{8,10},{9,11},{10,... | collective-permute-start | bytes 115976 | tf_op jit(solution)/shard_map/ppermute | solution.py:373
  205.0 2.9 %collective-permute-start.15 = (f32[19328]{0:T(1024)S(1)}, f32[19328]{0:T(1024)S(1)}, u32[]{:S(2)}, u32[]{:S(2)}) collective-permute-start(f32[19328]{0:T(1024)S(1)} %maximum_select_fusion.11), channel_id=1, source_target_pairs={{0,8},{4,12},{8,0},{12,4},{16,24},{20,28},{24,16},{28,20},{32,40},... | collective-permute-start | bytes 231944 | tf_op jit(solution)/shard_map/ppermute | solution.py:373
  211.6 2.4 collective-permute-done.16
  216.0 3.9 %collective-permute-done.17 = f32[77312]{0:T(1024)S(1)} collective-permute-done((f32[77312]{0:T(1024)S(1)}, f32[77312]{0:T(1024)S(1)}, u32[]{:S(2)}, u32[]{:S(2)}) %collective-permute-start.17) | collective-permute-done | bytes 309280 | tf_op jit(solution)/shard_map/ppermute | solution.py:373
  220.0 16.2 %collective-permute-start.18 = (f32[154624]{0:T(1024)S(1)}, f32[154624]{0:T(1024)S(1)}, u32[]{:S(2)}, u32[]{:S(2)}) collective-permute-start(f32[154624]{0:T(1024)S(1)} %maximum_select_fusion.3), channel_id=1, source_target_pairs={{0,128},{128,0},{1,129},{129,1},{2,130},{130,2},{3,131},{131,3},{4... | collective-permute-start | bytes 1855496 | tf_op jit(solution)/shard_map/ppermute | solution.py:373
  246.1 2.3 reshape.524
  248.4 2.0 reshape.525
  (203 shorter events, 68.8 us)
Async XLA Ops:
  0.6 14.1 %copy-start = (bf16[1,1,64,64,144]{4,3,2,1,0:T(8,128)(2,1)S(1)}, bf16[1,1,64,64,144]{4,3,2,1,0:T(8,128)(2,1)}, u32[]{:S(2)}) copy-start(bf16[1,1,64,64,144]{4,3,2,1,0:T(8,128)(2,1)} %param.12) | copy-start | bytes 3538948
  0.6 44.2 %collective-permute-start.1 = (bf16[1,100,12,256]{3,1,2,0:T(8,128)(2,1)}, bf16[1,100,12,256]{3,1,2,0:T(8,128)(2,1)S(1)}, u32[]{:S(2)}, u32[]{:S(2)}) collective-permute-start(bf16[1,100,12,256]{3,1,2,0:T(8,128)(2,1)} %param.10), channel_id=1, source_target_pairs={{4,0},{8,4},{12,8},{16,12},{20,16},{24,20},{28,24},{32,28},{36,32}... | collective-permute-start | bytes 1843208 | tf_op jit(solution)/shard_map/ppermute | solution.py:424
  3.5 41.3 %collective-permute-start = (bf16[1,100,1,256]{3,1,2,0:T(8,128)(2,1)}, bf16[1,100,1,256]{3,1,2,0:T(8,128)(2,1)}, u32[]{:S(2)}, u32[]{:S(2)}) collective-permute-start(bf16[1,100,1,256]{3,1,2,0:T(8,128)(2,1)} %slice.112), channel_id=1, source_target_pairs={{0,4},{4,8},{8,12},{12,16},{16,20},{20,24},{24,28},{28,32},{32,36}... | collective-permute-start | bytes 153608 | tf_op jit(solution)/shard_map/ppermute | solution.py:423
  10.4 33.3 %collective-permute-start.2 = (bf16[1,64,11,256]{3,1,2,0:T(8,128)(2,1)}, bf16[1,64,11,256]{3,1,2,0:T(8,128)(2,1)}, u32[]{:S(2)}, u32[]{:S(2)}) collective-permute-start(bf16[1,64,11,256]{3,1,2,0:T(8,128)(2,1)} %slice.115), channel_id=1, source_target_pairs={{4,0},{8,4},{12,8},{16,12},{20,16},{24,20},{28,24},{32,28},{36,32}... | collective-permute-start | bytes 1081352 | tf_op jit(solution)/shard_map/ppermute | solution.py:426
  19.9 17.3 %copy-start.14 = (bf16[128,900]{0,1:T(8,128)(2,1)S(1)}, bf16[128,900]{0,1:T(8,128)(2,1)}, u32[]{:S(2)}) copy-start(bf16[128,900]{0,1:T(8,128)(2,1)} %param.14) | copy-start | bytes 691204
  19.9 19.9 %copy-start.12 = (bf16[128,1152]{1,0:T(8,128)(2,1)S(1)}, bf16[128,1152]{1,0:T(8,128)(2,1)}, u32[]{:S(2)}) copy-start(bf16[128,1152]{1,0:T(8,128)(2,1)} %param.16) | copy-start | bytes 884740
  19.9 20.8 %copy-start.9 = (bf16[128,1152]{1,0:T(8,128)(2,1)S(1)}, bf16[128,1152]{1,0:T(8,128)(2,1)}, u32[]{:S(2)}) copy-start(bf16[128,1152]{1,0:T(8,128)(2,1)} %w2_ref.1) | copy-start | bytes 884740
  19.9 76.9 %all-to-all-start = ((bf16[32,2,64,144]{3,2,1,0:T(8,128)(2,1)}), bf16[32,2,64,144]{3,2,1,0:T(8,128)(2,1)}, u32[]{:S(2)}, u32[]{:S(2)}) async-start(bf16[32,2,64,144]{3,2,1,0:T(8,128)(2,1)} %broadcast_select_fusion), calls=%async_computation | async-start | bytes 4194304 | tf_op jit(solution)/shard_map/all_to_all | solution.py:421
  34.4 8.0 %copy-start.21 = (f32[32,128]{1,0:T(8,128)S(1)}, f32[32,128]{1,0:T(8,128)}, u32[]{:S(2)}) copy-start(f32[32,128]{1,0:T(8,128)} %param.19) | copy-start | bytes 49156
  34.4 9.3 %copy-start.8 = (bf16[1,64,12,256]{3,1,2,0:T(8,128)(2,1)S(1)}, bf16[1,64,12,256]{3,1,2,0:T(8,128)(2,1)}, u32[]{:S(2)}) copy-start(bf16[1,64,12,256]{3,1,2,0:T(8,128)(2,1)} %param.11) | copy-start | bytes 1179652
  36.5 8.4 %copy-start.15 = (f32[32,32]{1,0:T(8,128)}, f32[32,32]{1,0:T(8,128)S(1)}, u32[]{:S(2)}) copy-start(f32[32,32]{1,0:T(8,128)S(1)} %fusion.5) | copy-start | bytes 12292
  36.7 8.2 %copy-start.10 = (bf16[1,100,12,256]{3,1,2,0:T(8,128)(2,1)S(1)}, bf16[1,100,12,256]{3,1,2,0:T(8,128)(2,1)}, u32[]{:S(2)}) copy-start(bf16[1,100,12,256]{3,1,2,0:T(8,128)(2,1)} %param.10) | copy-start | bytes 1843204
  51.2 15.6 %copy-start.27 = (bf16[64,128]{1,0:T(8,128)(2,1)S(1)}, bf16[64,128]{1,0:T(8,128)(2,1)}, u32[]{:S(2)}) copy-start(bf16[64,128]{1,0:T(8,128)(2,1)} %param.15) | copy-start | bytes 49156
  146.9 3.7 %collective-permute-start.3 = (f32[154624]{0:T(1024)S(1)}, f32[154624]{0:T(1024)}, u32[]{:S(2)}, u32[]{:S(2)}) collective-permute-start(f32[154624]{0:T(1024)S(1)} %fusion.2), channel_id=1, source_target_pairs={{0,128},{128,0},{1,129},{129,1},{2,130},{130,2},{3,131},{131,3},{4... | collective-permute-start | bytes 1855496 | tf_op jit(solution)/shard_map/ppermute | solution.py:368
  151.8 56.0 %copy-start.7 = (bf16[23,256,64]{1,2,0:T(8,128)(2,1)S(1)}, bf16[23,256,64]{1,2,0:T(8,128)(2,1)}, u32[]{:S(2)}) copy-start(bf16[23,256,64]{1,2,0:T(8,128)(2,1)} %copy-done.6) | copy-start | bytes 2260996
  151.8 8.7 %collective-permute-start.4 = (f32[77312]{0:T(1024)S(1)}, f32[77312]{0:T(1024)S(1)}, u32[]{:S(2)}, u32[]{:S(2)}) collective-permute-start(f32[77312]{0:T(1024)S(1)} %slice_select_fusion), channel_id=1, source_target_pairs={{0,4},{4,0},{8,12},{12,8},{16,20},{20,16},{24,28},{28,24},{32,36},... | collective-permute-start | bytes 927752 | tf_op jit(solution)/shard_map/ppermute | solution.py:368
  160.6 4.2 %collective-permute-start.5 = (f32[38656]{0:T(1024)S(1)}, f32[38656]{0:T(1024)S(1)}, u32[]{:S(2)}, u32[]{:S(2)}) collective-permute-start(f32[38656]{0:T(1024)S(1)} %slice_select_fusion.1), channel_id=1, source_target_pairs={{0,1},{1,0},{2,3},{3,2},{4,5},{5,4},{6,7},{7,6},{8,9},{9,8},{10,11... | collective-permute-start | bytes 463880 | tf_op jit(solution)/shard_map/ppermute | solution.py:368
  164.8 4.8 %collective-permute-start.6 = (f32[19328]{0:T(1024)S(1)}, f32[19328]{0:T(1024)S(1)}, u32[]{:S(2)}, u32[]{:S(2)}) collective-permute-start(f32[19328]{0:T(1024)S(1)} %slice_select_fusion.2), channel_id=1, source_target_pairs={{0,8},{4,12},{8,0},{12,4},{16,24},{20,28},{24,16},{28,20},{32,40},... | collective-permute-start | bytes 231944 | tf_op jit(solution)/shard_map/ppermute | solution.py:368
  169.7 4.4 %collective-permute-start.7 = (f32[9664]{0:T(1024)S(1)}, f32[9664]{0:T(1024)S(1)}, u32[]{:S(2)}, u32[]{:S(2)}) collective-permute-start(f32[9664]{0:T(1024)S(1)} %slice_select_fusion.3), channel_id=1, source_target_pairs={{0,2},{1,3},{2,0},{3,1},{4,6},{5,7},{6,4},{7,5},{8,10},{9,11},{10,... | collective-permute-start | bytes 115976 | tf_op jit(solution)/shard_map/ppermute | solution.py:368
  174.4 2.7 %collective-permute-start.8 = (f32[4832]{0:T(1024)S(1)}, f32[4832]{0:T(1024)S(1)}, u32[]{:S(2)}, u32[]{:S(2)}) collective-permute-start(f32[4832]{0:T(1024)S(1)} %slice_select_fusion.4), channel_id=1, source_target_pairs={{0,16},{4,20},{8,24},{12,28},{16,0},{20,4},{24,8},{28,12},{32,48},... | collective-permute-start | bytes 57992 | tf_op jit(solution)/shard_map/ppermute | solution.py:368
  177.2 3.5 %collective-permute-start.9 = (f32[2416]{0:T(1024)S(1)}, f32[2416]{0:T(1024)S(1)}, u32[]{:S(2)}, u32[]{:S(2)}) collective-permute-start(f32[2416]{0:T(1024)S(1)} %slice_select_fusion.5), channel_id=1, source_target_pairs={{0,32},{4,36},{8,40},{12,44},{16,48},{20,52},{24,56},{28,60},{32,0... | collective-permute-start | bytes 29000 | tf_op jit(solution)/shard_map/ppermute | solution.py:368
  180.8 6.7 %collective-permute-start.10 = (f32[1208]{0:T(1024)S(1)}, f32[1208]{0:T(1024)S(1)}, u32[]{:S(2)}, u32[]{:S(2)}) collective-permute-start(f32[1208]{0:T(1024)S(1)} %slice_select_fusion.6), channel_id=1, source_target_pairs={{0,64},{4,68},{8,72},{12,76},{16,80},{20,84},{24,88},{28,92},{32,9... | collective-permute-start | bytes 14504 | tf_op jit(solution)/shard_map/ppermute | solution.py:368
  187.6 6.5 %collective-permute-start.11 = (f32[1208]{0:T(1024)S(1)}, f32[1208]{0:T(1024)S(1)}, u32[]{:S(2)}, u32[]{:S(2)}) collective-permute-start(f32[1208]{0:T(1024)S(1)} %select_add_fusion.7), channel_id=1, source_target_pairs={{0,64},{4,68},{8,72},{12,76},{16,80},{20,84},{24,88},{28,92},{32,9... | collective-permute-start | bytes 14504 | tf_op jit(solution)/shard_map/ppermute | solution.py:373
  194.2 3.5 %collective-permute-start.12 = (f32[2416]{0:T(1024)S(1)}, f32[2416]{0:T(1024)S(1)}, u32[]{:S(2)}, u32[]{:S(2)}) collective-permute-start(f32[2416]{0:T(1024)S(1)} %maximum_select_fusion.14), channel_id=1, source_target_pairs={{0,32},{4,36},{8,40},{12,44},{16,48},{20,52},{24,56},{28,60},{32,0... | collective-permute-start | bytes 29000 | tf_op jit(solution)/shard_map/ppermute | solution.py:373
  197.7 2.7 %collective-permute-start.13 = (f32[4832]{0:T(1024)S(1)}, f32[4832]{0:T(1024)S(1)}, u32[]{:S(2)}, u32[]{:S(2)}) collective-permute-start(f32[4832]{0:T(1024)S(1)} %maximum_select_fusion.13), channel_id=1, source_target_pairs={{0,16},{4,20},{8,24},{12,28},{16,0},{20,4},{24,8},{28,12},{32,48},... | collective-permute-start | bytes 57992 | tf_op jit(solution)/shard_map/ppermute | solution.py:373
  200.5 4.4 %collective-permute-start.14 = (f32[9664]{0:T(1024)S(1)}, f32[9664]{0:T(1024)S(1)}, u32[]{:S(2)}, u32[]{:S(2)}) collective-permute-start(f32[9664]{0:T(1024)S(1)} %maximum_select_fusion.12), channel_id=1, source_target_pairs={{0,2},{1,3},{2,0},{3,1},{4,6},{5,7},{6,4},{7,5},{8,10},{9,11},{10,... | collective-permute-start | bytes 115976 | tf_op jit(solution)/shard_map/ppermute | solution.py:373
  205.0 4.8 %collective-permute-start.15 = (f32[19328]{0:T(1024)S(1)}, f32[19328]{0:T(1024)S(1)}, u32[]{:S(2)}, u32[]{:S(2)}) collective-permute-start(f32[19328]{0:T(1024)S(1)} %maximum_select_fusion.11), channel_id=1, source_target_pairs={{0,8},{4,12},{8,0},{12,4},{16,24},{20,28},{24,16},{28,20},{32,40},... | collective-permute-start | bytes 231944 | tf_op jit(solution)/shard_map/ppermute | solution.py:373
  209.9 4.2 %collective-permute-start.16 = (f32[38656]{0:T(1024)S(1)}, f32[38656]{0:T(1024)S(1)}, u32[]{:S(2)}, u32[]{:S(2)}) collective-permute-start(f32[38656]{0:T(1024)S(1)} %maximum_select_fusion.9), channel_id=1, source_target_pairs={{0,1},{1,0},{2,3},{3,2},{4,5},{5,4},{6,7},{7,6},{8,9},{9,8},{10,11... | collective-permute-start | bytes 463880 | tf_op jit(solution)/shard_map/ppermute | solution.py:373
  214.1 5.8 %collective-permute-start.17 = (f32[77312]{0:T(1024)S(1)}, f32[77312]{0:T(1024)S(1)}, u32[]{:S(2)}, u32[]{:S(2)}) collective-permute-start(f32[77312]{0:T(1024)S(1)} %maximum_select_fusion.5), channel_id=1, source_target_pairs={{0,4},{4,0},{8,12},{12,8},{16,20},{20,16},{24,28},{28,24},{32,36},... | collective-permute-start | bytes 927752 | tf_op jit(solution)/shard_map/ppermute | solution.py:373
  220.0 17.8 %copy-start.5 = (f32[154624]{0:T(1024)}, f32[154624]{0:T(1024)S(1)}, u32[]{:S(2)}) copy-start(f32[154624]{0:T(1024)S(1)} %maximum_select_fusion.3) | copy-start | bytes 1855492
  220.0 18.9 %collective-permute-start.18 = (f32[154624]{0:T(1024)S(1)}, f32[154624]{0:T(1024)S(1)}, u32[]{:S(2)}, u32[]{:S(2)}) collective-permute-start(f32[154624]{0:T(1024)S(1)} %maximum_select_fusion.3), channel_id=1, source_target_pairs={{0,128},{128,0},{1,129},{129,1},{2,130},{130,2},{3,131},{131,3},{4... | collective-permute-start | bytes 1855496 | tf_op jit(solution)/shard_map/ppermute | solution.py:373
  245.0 8.7 %copy-start.1 = (bf16[1,1,64,64,144]{4,3,2,1,0:T(8,128)(2,1)S(1)}, bf16[1,1,64,64,144]{4,3,2,1,0:T(8,128)(2,1)}, u32[]{:S(2)}) copy-start(bf16[1,1,64,64,144]{4,3,2,1,0:T(8,128)(2,1)} %param.12) | copy-start | bytes 3538948
  (16 other events, 59.1 us)
where the time goes:
time: 260 us; the launch traced here: 255 us
  starting transfers between devices  76.4 us (29%)
  local copies, waits for them, and re-layouts  72.4 us (28%)
  waiting for transfers between devices  30.6 us (12%)
  Pallas kernels  29 us (11%)
  other arithmetic  24.6 us (9%)
  matrix products  16.7 us (6%)
  between operations  5.27 us (2%)
    ppermute x8, starting transfers between devices, exchange_sum(): other = lax.ppermute(values, axis, route)  33.7 us
    pallas_call x1, Pallas kernels, patch_pass(): pl.pallas_call(patch_kernel, grid=(steps,), in_specs=[block((rows, channe...  29 us
    ppermute x8, starting transfers between devices, exchange_sum(): values = kept + lax.ppermute(sent, axis, route)  20.4 us
    ppermute x8, waiting for transfers between devices, exchange_sum(): values = kept + lax.ppermute(sent, axis, route)  18.3 us
    conv_general_dilated x1, matrix products, regress(): lax.conv_general_dilated(grid_rows[None], kernel, window_strides=(1, 1),...  15.6 us
    all_to_all x1, starting transfers between devices, per_device(): lax.all_to_all(outgoing, 'rows', split_axis=0, concat_axis=0, tiled=True)  14.4 us
    unnamed x67, local copies, waits for them, and re-layouts  12.8 us
    ppermute x8, waiting for transfers between devices, exchange_sum(): other = lax.ppermute(values, axis, route)  12.3 us
  transfers between devices with their start and end apart: 20, of which 15 were waited for; matrix products, arithmetic and copies ran while one was open for 30% of the time, Pallas kernels for 0%

commit v1 on v0

--- a/solution.py
+++ b/solution.py
@@ -243,7 +243,7 @@
         sums_ref[group : group + 1, :] = jnp.sum(wide[group * cells : (group + 1) * cells], axis=0, keepdims=True)
 
 
-def patch_pass(xin, skip, scale, emb, conv_one, conv_two, out_proj, group=8, interpret=False):
+def patch_pass(xin, skip, scale, emb, conv_one, conv_two, out_proj, group=16, interpret=False):
     rows_all, channels = xin.shape
     cells = PATCH * PATCH
     patches = rows_all // cells

time: 260 us -> 261 us (level)
  transfers between devices with their start and end apart: 20 -> 20, of which waited for: 15 -> 15; matrix products, arithmetic and copies ran while one was open for 30% -> 31% of each run, Pallas kernels for 0% -> 0%
where the time goes in v1:
time: 261 us; the launch traced here: 255 us
  starting transfers between devices  76.3 us (29%)
  local copies, waits for them, and re-layouts  73 us (28%)
  waiting for transfers between devices  30.6 us (12%)
  Pallas kernels  28.5 us (11%)
  other arithmetic  25.1 us (10%)
  matrix products  16.7 us (6%)
  between operations  5.29 us (2%)
    ppermute x8, starting transfers between devices, exchange_sum(): other = lax.ppermute(values, axis, route)  33.9 us
    pallas_call x1, Pallas kernels, patch_pass(): pl.pallas_call(patch_kernel, grid=(steps,), in_specs=[block((rows, channe...  28.5 us
    ppermute x8, starting transfers between devices, exchange_sum(): values = kept + lax.ppermute(sent, axis, route)  20.1 us
    ppermute x8, waiting for transfers between devices, exchange_sum(): values = kept + lax.ppermute(sent, axis, route)  18.4 us
    conv_general_dilated x1, matrix products, regress(): lax.conv_general_dilated(grid_rows[None], kernel, window_strides=(1, 1),...  15.6 us
    all_to_all x1, starting transfers between devices, per_device(): lax.all_to_all(outgoing, 'rows', split_axis=0, concat_axis=0, tiled=True)  14.4 us
    unnamed x67, local copies, waits for them, and re-layouts  12.8 us
    ppermute x8, waiting for transfers between devices, exchange_sum(): other = lax.ppermute(values, axis, route)  12.2 us
  transfers between devices with their start and end apart: 20, of which 15 were waited for; matrix products, arithmetic and copies ran while one was open for 31% of the time, Pallas kernels for 0%

profile of v1, /device:TPU:1, one launch (start us, length us, event | category | flops | bytes accessed | tf_op | source)
XLA Modules:
  0.0 255.4 jit_solution(8702424355419249364)
XLA Ops:
  3.5 5.2 %collective-permute-start = (bf16[1,100,1,256]{3,1,2,0:T(8,128)(2,1)}, bf16[1,100,1,256]{3,1,2,0:T(8,128)(2,1)}, u32[]{:S(2)}, u32[]{:S(2)}) collective-permute-start(bf16[1,100,1,256]{3,1,2,0:T(8,128)(2,1)} %slice.112), channel_id=1, source_target_pairs={{0,4},{4,8},{8,12},{12,16},{16,20},{20,24},{24,28},{28,32},{32,36}... | collective-permute-start | bytes 153608 | tf_op jit(solution)/shard_map/ppermute | solution.py:423
  14.7 2.0 gather_fusion.1
  16.8 3.2 %broadcast_select_fusion = bf16[32,2,64,144]{3,2,1,0:T(8,128)(2,1)} fusion(bf16[32,2,64,144]{3,2,1,0:T(8,128)(2,1)} %bitcast.93, pred[32,2]{1,0:T(8,128)(4,1)S(1)} %copy.68), kind=kLoop, calls=%fused_computation.10 | loop fusion | flops 589824 | bytes 2359360 | tf_op jit(solution)/shard_map/jit(_take)/select_n | solution.py:419
  20.0 14.4 %all-to-all-start = ((bf16[32,2,64,144]{3,2,1,0:T(8,128)(2,1)}), bf16[32,2,64,144]{3,2,1,0:T(8,128)(2,1)}, u32[]{:S(2)}, u32[]{:S(2)}) async-start(bf16[32,2,64,144]{3,2,1,0:T(8,128)(2,1)} %broadcast_select_fusion), calls=%async_computation | async-start | bytes 4194304 | tf_op jit(solution)/shard_map/all_to_all | solution.py:421
  46.8 5.4 %copy.63 = bf16[1,100,25,256]{1,0,3,2:T(2,128)(2,1)} copy(bf16[1,100,25,256]{3,1,2,0:T(8,128)(2,1)S(1)} %pad_maximum_fusion.1) | data formatting | bytes 2560000 | tf_op jit(solution)/shard_map/concatenate | solution.py:427
  52.3 15.6 %fusion.20 = f32[1,23,256,128]{3,0,2,1:T(1,128)S(1)} fusion(bf16[1,100,25,256]{1,0,3,2:T(2,128)(2,1)} %copy.63, bf16[128,3,3,100]{0,3,2,1:T(8,128)(2,1)S(1)} %copy-done.13), kind=kOutput, calls=%fused_computation.136 | convolution fusion | flops 1353062400 | bytes 4525056 | tf_op jit(solution)/shard_map/conv_general_dilated | solution.py:84
  70.0 5.5 %copy.64 = bf16[2,64,23,256]{1,0,3,2:T(2,128)(2,1)} copy(bf16[2,64,23,256]{3,1,2,0:T(8,128)(2,1)S(1)} %pad_maximum_fusion) | data formatting | bytes 3014656 | tf_op jit(solution)/shard_map/stack | solution.py:432
  75.5 8.6 %gather_fusion = bf16[32,2,64,12,12]{2,1,4,3,0:T(2,128)(2,1)S(1)} fusion(bf16[2,64,23,256]{1,0,3,2:T(2,128)(2,1)} %copy.64, s32[32]{0:T(128)S(1)} %get-tuple-element.43), kind=kCustom, calls=%fused_computation | custom fusion | bytes 2359808 | tf_op jit(solution)/shard_map/vmap()/gather | solution.py:396
  84.2 5.4 %fusion.18 = (bf16[32,1,64,144]{2,1,3,0:T(2,128)(2,1)}, bf16[32,1,64,144]{2,1,3,0:T(2,128)(2,1)}) fusion(bf16[32,2,64,144]{2,1,3,0:T(2,128)(2,1)S(1)} %bitcast.88), kind=kLoop, calls=%fused_computation.134 | loop fusion | bytes 2359296 | tf_op jit(solution)/shard_map/slice | solution.py:438
  89.6 4.8 %copy.89 = bf16[32,1,64,144]{3,2,0,1:T(8,128)(2,1)S(1)} copy(bf16[32,1,64,144]{2,1,3,0:T(2,128)(2,1)} %get-tuple-element.35) | data formatting | bytes 1179648
  94.4 3.4 %copy.88 = bf16[32,1,64,144]{3,2,0,1:T(8,128)(2,1)} copy(bf16[32,1,64,144]{2,1,3,0:T(2,128)(2,1)S(1)} %copy-done.2) | data formatting | bytes 1179648
  97.9 3.2 %gather_fusion.2 = bf16[32,64,144]{2,1,0:T(8,128)(2,1)} fusion(bf16[64,64,144]{2,1,0:T(8,128)(2,1)} %bitcast.23, s32[1024]{0:T(1024)S(1)} %pad_clamp_fusion), kind=kCustom, calls=%fused_computation.2 | custom fusion | bytes 1179776 | tf_op jit(solution)/shard_map/jit(_take)/gather | solution.py:435
  101.1 2.4 subtract_bitcast_fusion
  105.2 3.8 %copy.70 = bf16[32,144,128]{2,1,0:T(8,128)(2,1)} copy(bf16[32,144,128]{1,2,0:T(8,128)(2,1)} %maximum_bitcast_fusion) | data formatting | bytes 2359296 | tf_op jit(solution)/shard_map/transpose | solution.py:311
  109.0 2.1 copy.71
  114.4 28.5 %shard_map.145 = (f32[4608,64]{1,0:T(8,128)}, f32[32,128]{1,0:T(8,128)}, f32[128,1152]{1,0:T(8,128)}, f32[128,1152]{1,0:T(8,128)}, f32[64,128]{1,0:T(8,128)}) custom-call(bf16[4608,128]{1,0:T(8,128)(2,1)} %bitcast.95, f32[4608,64]{1,0:T(8,128)} %bitcast.89, f32[4608,8]{1,0:T(8,128)} %bitcast.90, f32[4608,128]{1,0:T(8,128)} %bitcast.91, ...), custom_call_target="tpu_custom_call" | custom-call | tf_op jit(solution)/shard_map/pallas_call | solution.py:258
  144.5 2.3 multiply_reduce_fusion
  153.9 7.1 %collective-permute-done.4 = f32[77312]{0:T(1024)S(1)} collective-permute-done((f32[77312]{0:T(1024)S(1)}, f32[77312]{0:T(1024)S(1)}, u32[]{:S(2)}, u32[]{:S(2)}) %collective-permute-start.4) | collective-permute-done | bytes 309280 | tf_op jit(solution)/shard_map/ppermute | solution.py:368
  162.5 2.8 %collective-permute-done.5 = f32[38656]{0:T(1024)S(1)} collective-permute-done((f32[38656]{0:T(1024)S(1)}, f32[38656]{0:T(1024)S(1)}, u32[]{:S(2)}, u32[]{:S(2)}) %collective-permute-start.5) | collective-permute-done | bytes 154656 | tf_op jit(solution)/shard_map/ppermute | solution.py:368
  165.3 3.0 %collective-permute-start.6 = (f32[19328]{0:T(1024)S(1)}, f32[19328]{0:T(1024)S(1)}, u32[]{:S(2)}, u32[]{:S(2)}) collective-permute-start(f32[19328]{0:T(1024)S(1)} %slice_select_fusion.2), channel_id=1, source_target_pairs={{0,8},{4,12},{8,0},{12,4},{16,24},{20,28},{24,16},{28,20},{32,40},... | collective-permute-start | bytes 231944 | tf_op jit(solution)/shard_map/ppermute | solution.py:368
  170.3 3.0 %collective-permute-start.7 = (f32[9664]{0:T(1024)S(1)}, f32[9664]{0:T(1024)S(1)}, u32[]{:S(2)}, u32[]{:S(2)}) collective-permute-start(f32[9664]{0:T(1024)S(1)} %slice_select_fusion.3), channel_id=1, source_target_pairs={{0,2},{1,3},{2,0},{3,1},{4,6},{5,7},{6,4},{7,5},{8,10},{9,11},{10,... | collective-permute-start | bytes 115976 | tf_op jit(solution)/shard_map/ppermute | solution.py:368
  177.7 2.4 collective-permute-start.9
  181.3 5.5 %collective-permute-start.10 = (f32[1208]{0:T(1024)S(1)}, f32[1208]{0:T(1024)S(1)}, u32[]{:S(2)}, u32[]{:S(2)}) collective-permute-start(f32[1208]{0:T(1024)S(1)} %slice_select_fusion.6), channel_id=1, source_target_pairs={{0,64},{4,68},{8,72},{12,76},{16,80},{20,84},{24,88},{28,92},{32,9... | collective-permute-start | bytes 14504 | tf_op jit(solution)/shard_map/ppermute | solution.py:368
  188.0 5.5 %collective-permute-start.11 = (f32[1208]{0:T(1024)S(1)}, f32[1208]{0:T(1024)S(1)}, u32[]{:S(2)}, u32[]{:S(2)}) collective-permute-start(f32[1208]{0:T(1024)S(1)} %select_add_fusion.7), channel_id=1, source_target_pairs={{0,64},{4,68},{8,72},{12,76},{16,80},{20,84},{24,88},{28,92},{32,9... | collective-permute-start | bytes 14504 | tf_op jit(solution)/shard_map/ppermute | solution.py:373
  194.5 2.3 collective-permute-start.12
  200.8 3.0 %collective-permute-start.14 = (f32[9664]{0:T(1024)S(1)}, f32[9664]{0:T(1024)S(1)}, u32[]{:S(2)}, u32[]{:S(2)}) collective-permute-start(f32[9664]{0:T(1024)S(1)} %maximum_select_fusion.12), channel_id=1, source_target_pairs={{0,2},{1,3},{2,0},{3,1},{4,6},{5,7},{6,4},{7,5},{8,10},{9,11},{10,... | collective-permute-start | bytes 115976 | tf_op jit(solution)/shard_map/ppermute | solution.py:373
  205.4 2.9 %collective-permute-start.15 = (f32[19328]{0:T(1024)S(1)}, f32[19328]{0:T(1024)S(1)}, u32[]{:S(2)}, u32[]{:S(2)}) collective-permute-start(f32[19328]{0:T(1024)S(1)} %maximum_select_fusion.11), channel_id=1, source_target_pairs={{0,8},{4,12},{8,0},{12,4},{16,24},{20,28},{24,16},{28,20},{32,40},... | collective-permute-start | bytes 231944 | tf_op jit(solution)/shard_map/ppermute | solution.py:373
  212.0 2.4 collective-permute-done.16
  216.4 3.9 %collective-permute-done.17 = f32[77312]{0:T(1024)S(1)} collective-permute-done((f32[77312]{0:T(1024)S(1)}, f32[77312]{0:T(1024)S(1)}, u32[]{:S(2)}, u32[]{:S(2)}) %collective-permute-start.17) | collective-permute-done | bytes 309280 | tf_op jit(solution)/shard_map/ppermute | solution.py:373
  220.4 16.3 %collective-permute-start.18 = (f32[154624]{0:T(1024)S(1)}, f32[154624]{0:T(1024)S(1)}, u32[]{:S(2)}, u32[]{:S(2)}) collective-permute-start(f32[154624]{0:T(1024)S(1)} %maximum_select_fusion.3), channel_id=1, source_target_pairs={{0,128},{128,0},{1,129},{129,1},{2,130},{130,2},{3,131},{131,3},{4... | collective-permute-start | bytes 1855496 | tf_op jit(solution)/shard_map/ppermute | solution.py:373
  246.5 2.3 reshape.524
  248.8 2.0 reshape.525
  (203 shorter events, 69.9 us)
Async XLA Ops:
  0.6 14.1 %copy-start = (bf16[1,1,64,64,144]{4,3,2,1,0:T(8,128)(2,1)S(1)}, bf16[1,1,64,64,144]{4,3,2,1,0:T(8,128)(2,1)}, u32[]{:S(2)}) copy-start(bf16[1,1,64,64,144]{4,3,2,1,0:T(8,128)(2,1)} %param.12) | copy-start | bytes 3538948
  0.6 45.2 %collective-permute-start.1 = (bf16[1,100,12,256]{3,1,2,0:T(8,128)(2,1)}, bf16[1,100,12,256]{3,1,2,0:T(8,128)(2,1)S(1)}, u32[]{:S(2)}, u32[]{:S(2)}) collective-permute-start(bf16[1,100,12,256]{3,1,2,0:T(8,128)(2,1)} %param.10), channel_id=1, source_target_pairs={{4,0},{8,4},{12,8},{16,12},{20,16},{24,20},{28,24},{32,28},{36,32}... | collective-permute-start | bytes 1843208 | tf_op jit(solution)/shard_map/ppermute | solution.py:424
  3.5 42.3 %collective-permute-start = (bf16[1,100,1,256]{3,1,2,0:T(8,128)(2,1)}, bf16[1,100,1,256]{3,1,2,0:T(8,128)(2,1)}, u32[]{:S(2)}, u32[]{:S(2)}) collective-permute-start(bf16[1,100,1,256]{3,1,2,0:T(8,128)(2,1)} %slice.112), channel_id=1, source_target_pairs={{0,4},{4,8},{8,12},{12,16},{16,20},{20,24},{24,28},{28,32},{32,36}... | collective-permute-start | bytes 153608 | tf_op jit(solution)/shard_map/ppermute | solution.py:423
  10.5 34.3 %collective-permute-start.2 = (bf16[1,64,11,256]{3,1,2,0:T(8,128)(2,1)}, bf16[1,64,11,256]{3,1,2,0:T(8,128)(2,1)}, u32[]{:S(2)}, u32[]{:S(2)}) collective-permute-start(bf16[1,64,11,256]{3,1,2,0:T(8,128)(2,1)} %slice.115), channel_id=1, source_target_pairs={{4,0},{8,4},{12,8},{16,12},{20,16},{24,20},{28,24},{32,28},{36,32}... | collective-permute-start | bytes 1081352 | tf_op jit(solution)/shard_map/ppermute | solution.py:426
  20.0 17.8 %copy-start.14 = (bf16[128,900]{0,1:T(8,128)(2,1)S(1)}, bf16[128,900]{0,1:T(8,128)(2,1)}, u32[]{:S(2)}) copy-start(bf16[128,900]{0,1:T(8,128)(2,1)} %param.14) | copy-start | bytes 691204
  20.0 77.9 %all-to-all-start = ((bf16[32,2,64,144]{3,2,1,0:T(8,128)(2,1)}), bf16[32,2,64,144]{3,2,1,0:T(8,128)(2,1)}, u32[]{:S(2)}, u32[]{:S(2)}) async-start(bf16[32,2,64,144]{3,2,1,0:T(8,128)(2,1)} %broadcast_select_fusion), calls=%async_computation | async-start | bytes 4194304 | tf_op jit(solution)/shard_map/all_to_all | solution.py:421
  34.4 7.3 %copy-start.9 = (bf16[128,1152]{1,0:T(8,128)(2,1)S(1)}, bf16[128,1152]{1,0:T(8,128)(2,1)}, u32[]{:S(2)}) copy-start(bf16[128,1152]{1,0:T(8,128)(2,1)} %w2_ref.1) | copy-start | bytes 884740
  34.4 8.3 %copy-start.17 = (bf16[64,128]{1,0:T(8,128)(2,1)S(1)}, bf16[64,128]{1,0:T(8,128)(2,1)}, u32[]{:S(2)}) copy-start(bf16[64,128]{1,0:T(8,128)(2,1)} %pm_ref.1) | copy-start | bytes 49156
  34.4 9.0 %copy-start.21 = (f32[32,128]{1,0:T(8,128)S(1)}, f32[32,128]{1,0:T(8,128)}, u32[]{:S(2)}) copy-start(f32[32,128]{1,0:T(8,128)} %param.19) | copy-start | bytes 49156
  34.5 10.3 %copy-start.8 = (bf16[1,64,12,256]{3,1,2,0:T(8,128)(2,1)S(1)}, bf16[1,64,12,256]{3,1,2,0:T(8,128)(2,1)}, u32[]{:S(2)}) copy-start(bf16[1,64,12,256]{3,1,2,0:T(8,128)(2,1)} %param.11) | copy-start | bytes 1179652
  37.0 8.8 %copy-start.15 = (f32[32,32]{1,0:T(8,128)}, f32[32,32]{1,0:T(8,128)S(1)}, u32[]{:S(2)}) copy-start(f32[32,32]{1,0:T(8,128)S(1)} %fusion.5) | copy-start | bytes 12292
  52.3 15.6 %copy-start.27 = (bf16[64,128]{1,0:T(8,128)(2,1)S(1)}, bf16[64,128]{1,0:T(8,128)(2,1)}, u32[]{:S(2)}) copy-start(bf16[64,128]{1,0:T(8,128)(2,1)} %param.15) | copy-start | bytes 49156
  94.4 6.7 %copy-start.23 = (f32[32]{0:T(128)S(1)}, f32[32]{0:T(128)}, u32[]{:S(2)}) copy-start(f32[32]{0:T(128)} %get-tuple-element.47) | copy-start | bytes 388
  147.5 3.7 %collective-permute-start.3 = (f32[154624]{0:T(1024)S(1)}, f32[154624]{0:T(1024)}, u32[]{:S(2)}, u32[]{:S(2)}) collective-permute-start(f32[154624]{0:T(1024)S(1)} %fusion.2), channel_id=1, source_target_pairs={{0,128},{128,0},{1,129},{129,1},{2,130},{130,2},{3,131},{131,3},{4... | collective-permute-start | bytes 1855496 | tf_op jit(solution)/shard_map/ppermute | solution.py:368
  152.4 55.8 %copy-start.7 = (bf16[23,256,64]{1,2,0:T(8,128)(2,1)S(1)}, bf16[23,256,64]{1,2,0:T(8,128)(2,1)}, u32[]{:S(2)}) copy-start(bf16[23,256,64]{1,2,0:T(8,128)(2,1)} %copy-done.6) | copy-start | bytes 2260996
  152.4 8.7 %collective-permute-start.4 = (f32[77312]{0:T(1024)S(1)}, f32[77312]{0:T(1024)S(1)}, u32[]{:S(2)}, u32[]{:S(2)}) collective-permute-start(f32[77312]{0:T(1024)S(1)} %slice_select_fusion), channel_id=1, source_target_pairs={{0,4},{4,0},{8,12},{12,8},{16,20},{20,16},{24,28},{28,24},{32,36},... | collective-permute-start | bytes 927752 | tf_op jit(solution)/shard_map/ppermute | solution.py:368
  161.1 4.2 %collective-permute-start.5 = (f32[38656]{0:T(1024)S(1)}, f32[38656]{0:T(1024)S(1)}, u32[]{:S(2)}, u32[]{:S(2)}) collective-permute-start(f32[38656]{0:T(1024)S(1)} %slice_select_fusion.1), channel_id=1, source_target_pairs={{0,1},{1,0},{2,3},{3,2},{4,5},{5,4},{6,7},{7,6},{8,9},{9,8},{10,11... | collective-permute-start | bytes 463880 | tf_op jit(solution)/shard_map/ppermute | solution.py:368
  165.3 4.8 %collective-permute-start.6 = (f32[19328]{0:T(1024)S(1)}, f32[19328]{0:T(1024)S(1)}, u32[]{:S(2)}, u32[]{:S(2)}) collective-permute-start(f32[19328]{0:T(1024)S(1)} %slice_select_fusion.2), channel_id=1, source_target_pairs={{0,8},{4,12},{8,0},{12,4},{16,24},{20,28},{24,16},{28,20},{32,40},... | collective-permute-start | bytes 231944 | tf_op jit(solution)/shard_map/ppermute | solution.py:368
  170.3 4.4 %collective-permute-start.7 = (f32[9664]{0:T(1024)S(1)}, f32[9664]{0:T(1024)S(1)}, u32[]{:S(2)}, u32[]{:S(2)}) collective-permute-start(f32[9664]{0:T(1024)S(1)} %slice_select_fusion.3), channel_id=1, source_target_pairs={{0,2},{1,3},{2,0},{3,1},{4,6},{5,7},{6,4},{7,5},{8,10},{9,11},{10,... | collective-permute-start | bytes 115976 | tf_op jit(solution)/shard_map/ppermute | solution.py:368
  174.9 2.7 %collective-permute-start.8 = (f32[4832]{0:T(1024)S(1)}, f32[4832]{0:T(1024)S(1)}, u32[]{:S(2)}, u32[]{:S(2)}) collective-permute-start(f32[4832]{0:T(1024)S(1)} %slice_select_fusion.4), channel_id=1, source_target_pairs={{0,16},{4,20},{8,24},{12,28},{16,0},{20,4},{24,8},{28,12},{32,48},... | collective-permute-start | bytes 57992 | tf_op jit(solution)/shard_map/ppermute | solution.py:368
  177.7 3.5 %collective-permute-start.9 = (f32[2416]{0:T(1024)S(1)}, f32[2416]{0:T(1024)S(1)}, u32[]{:S(2)}, u32[]{:S(2)}) collective-permute-start(f32[2416]{0:T(1024)S(1)} %slice_select_fusion.5), channel_id=1, source_target_pairs={{0,32},{4,36},{8,40},{12,44},{16,48},{20,52},{24,56},{28,60},{32,0... | collective-permute-start | bytes 29000 | tf_op jit(solution)/shard_map/ppermute | solution.py:368
  181.3 6.5 %collective-permute-start.10 = (f32[1208]{0:T(1024)S(1)}, f32[1208]{0:T(1024)S(1)}, u32[]{:S(2)}, u32[]{:S(2)}) collective-permute-start(f32[1208]{0:T(1024)S(1)} %slice_select_fusion.6), channel_id=1, source_target_pairs={{0,64},{4,68},{8,72},{12,76},{16,80},{20,84},{24,88},{28,92},{32,9... | collective-permute-start | bytes 14504 | tf_op jit(solution)/shard_map/ppermute | solution.py:368
  188.0 6.5 %collective-permute-start.11 = (f32[1208]{0:T(1024)S(1)}, f32[1208]{0:T(1024)S(1)}, u32[]{:S(2)}, u32[]{:S(2)}) collective-permute-start(f32[1208]{0:T(1024)S(1)} %select_add_fusion.7), channel_id=1, source_target_pairs={{0,64},{4,68},{8,72},{12,76},{16,80},{20,84},{24,88},{28,92},{32,9... | collective-permute-start | bytes 14504 | tf_op jit(solution)/shard_map/ppermute | solution.py:373
  194.5 3.5 %collective-permute-start.12 = (f32[2416]{0:T(1024)S(1)}, f32[2416]{0:T(1024)S(1)}, u32[]{:S(2)}, u32[]{:S(2)}) collective-permute-start(f32[2416]{0:T(1024)S(1)} %maximum_select_fusion.14), channel_id=1, source_target_pairs={{0,32},{4,36},{8,40},{12,44},{16,48},{20,52},{24,56},{28,60},{32,0... | collective-permute-start | bytes 29000 | tf_op jit(solution)/shard_map/ppermute | solution.py:373
  198.1 2.7 %collective-permute-start.13 = (f32[4832]{0:T(1024)S(1)}, f32[4832]{0:T(1024)S(1)}, u32[]{:S(2)}, u32[]{:S(2)}) collective-permute-start(f32[4832]{0:T(1024)S(1)} %maximum_select_fusion.13), channel_id=1, source_target_pairs={{0,16},{4,20},{8,24},{12,28},{16,0},{20,4},{24,8},{28,12},{32,48},... | collective-permute-start | bytes 57992 | tf_op jit(solution)/shard_map/ppermute | solution.py:373
  200.8 4.4 %collective-permute-start.14 = (f32[9664]{0:T(1024)S(1)}, f32[9664]{0:T(1024)S(1)}, u32[]{:S(2)}, u32[]{:S(2)}) collective-permute-start(f32[9664]{0:T(1024)S(1)} %maximum_select_fusion.12), channel_id=1, source_target_pairs={{0,2},{1,3},{2,0},{3,1},{4,6},{5,7},{6,4},{7,5},{8,10},{9,11},{10,... | collective-permute-start | bytes 115976 | tf_op jit(solution)/shard_map/ppermute | solution.py:373
  205.4 4.8 %collective-permute-start.15 = (f32[19328]{0:T(1024)S(1)}, f32[19328]{0:T(1024)S(1)}, u32[]{:S(2)}, u32[]{:S(2)}) collective-permute-start(f32[19328]{0:T(1024)S(1)} %maximum_select_fusion.11), channel_id=1, source_target_pairs={{0,8},{4,12},{8,0},{12,4},{16,24},{20,28},{24,16},{28,20},{32,40},... | collective-permute-start | bytes 231944 | tf_op jit(solution)/shard_map/ppermute | solution.py:373
  210.2 4.2 %collective-permute-start.16 = (f32[38656]{0:T(1024)S(1)}, f32[38656]{0:T(1024)S(1)}, u32[]{:S(2)}, u32[]{:S(2)}) collective-permute-start(f32[38656]{0:T(1024)S(1)} %maximum_select_fusion.9), channel_id=1, source_target_pairs={{0,1},{1,0},{2,3},{3,2},{4,5},{5,4},{6,7},{7,6},{8,9},{9,8},{10,11... | collective-permute-start | bytes 463880 | tf_op jit(solution)/shard_map/ppermute | solution.py:373
  214.5 5.8 %collective-permute-start.17 = (f32[77312]{0:T(1024)S(1)}, f32[77312]{0:T(1024)S(1)}, u32[]{:S(2)}, u32[]{:S(2)}) collective-permute-start(f32[77312]{0:T(1024)S(1)} %maximum_select_fusion.5), channel_id=1, source_target_pairs={{0,4},{4,0},{8,12},{12,8},{16,20},{20,16},{24,28},{28,24},{32,36},... | collective-permute-start | bytes 927752 | tf_op jit(solution)/shard_map/ppermute | solution.py:373
  220.4 17.8 %copy-start.5 = (f32[154624]{0:T(1024)}, f32[154624]{0:T(1024)S(1)}, u32[]{:S(2)}) copy-start(f32[154624]{0:T(1024)S(1)} %maximum_select_fusion.3) | copy-start | bytes 1855492
  220.4 19.0 %collective-permute-start.18 = (f32[154624]{0:T(1024)S(1)}, f32[154624]{0:T(1024)S(1)}, u32[]{:S(2)}, u32[]{:S(2)}) collective-permute-start(f32[154624]{0:T(1024)S(1)} %maximum_select_fusion.3), channel_id=1, source_target_pairs={{0,128},{128,0},{1,129},{129,1},{2,130},{130,2},{3,131},{131,3},{4... | collective-permute-start | bytes 1855496 | tf_op jit(solution)/shard_map/ppermute | solution.py:373
  245.4 8.7 %copy-start.1 = (bf16[1,1,64,64,144]{4,3,2,1,0:T(8,128)(2,1)S(1)}, bf16[1,1,64,64,144]{4,3,2,1,0:T(8,128)(2,1)}, u32[]{:S(2)}) copy-start(bf16[1,1,64,64,144]{4,3,2,1,0:T(8,128)(2,1)} %param.12) | copy-start | bytes 3538948
  (16 other events, 58.2 us)

commit v2 on v0

--- a/solution.py
+++ b/solution.py
@@ -360,20 +360,20 @@
     for axis, distance in steps:
         count = lax.axis_size(axis)
         half = values.shape[0] // 2
-        low, high = values[:half], values[half:]
-        upper = (places[axis] // distance) % 2 == 1
+        upper = (places[axis] // distance) % 2
         route = [(i, i ^ distance) for i in range(count)]
-        kept = jnp.where(upper, high, low)
-        sent = jnp.where(upper, low, high)
+        kept = lax.dynamic_slice_in_dim(values, upper * half, half)
+        sent = lax.dynamic_slice_in_dim(values, (1 - upper) * half, half)
         values = kept + lax.ppermute(sent, axis, route)
     for axis, distance in reversed(steps):
         count = lax.axis_size(axis)
-        upper = (places[axis] // distance) % 2 == 1
+        upper = (places[axis] // distance) % 2
         route = [(i, i ^ distance) for i in range(count)]
         other = lax.ppermute(values, axis, route)
-        values = jnp.where(
-            upper, jnp.concatenate([other, values]), jnp.concatenate([values, other])
-        )
+        width = values.shape[0]
+        joined = jnp.zeros((2 * width,), values.dtype)
+        joined = lax.dynamic_update_slice_in_dim(joined, values, upper * width, 0)
+        values = lax.dynamic_update_slice_in_dim(joined, other, (1 - upper) * width, 0)
     return values[:size]
 
 

time: 260 us -> 302 us (1.16)
  waiting for transfers between devices: 30.6 us -> 59.5 us
  starting transfers between devices: 76.4 us -> 90.9 us
  local copies, waits for them, and re-layouts: 72.4 us -> 82.2 us
  other arithmetic: 24.6 us -> 16.6 us
  between operations: 5.27 us -> 1.52 us
    ppermute x1, waiting for transfers between devices: 0.01 us -> 26.8 us  [per_device(): lax.ppermute(target[:, :, :height - 1], 'rows', [(i + 1, i) for i in rang...]
    ppermute x8, starting transfers between devices: 20.4 us -> 41.7 us  [exchange_sum(): values = kept + lax.ppermute(sent, axis, route)]
    dynamic_update_slice x0 -> x15, local copies, waits for them, and re-layouts: none -> 18.6 us  [the longest x7 9.55 us: exchange_sum(): joined = lax.dynamic_update_slice_in_dim(joined, values, upper * width, 0)]
    select_n x23 -> x0, other arithmetic: 6.06 us -> none  [the longest x15 5.62 us: exchange_sum(): jnp.where(upper, jnp.concatenate([other, values]), jnp.concatenate([value...]
    ppermute x8, starting transfers between devices: 33.7 us -> 29.8 us  [exchange_sum(): other = lax.ppermute(values, axis, route)]
    concatenate x10 -> x0, local copies, waits for them, and re-layouts: 3.64 us -> none  [exchange_sum(): jnp.concatenate([other, values])]
    unnamed x67 -> x61, local copies, waits for them, and re-layouts: 12.8 us -> 12.9 us
  transfers between devices with their start and end apart: 20 -> 20, of which waited for: 15 -> 16; matrix products, arithmetic and copies ran while one was open for 30% -> 24% of each run, Pallas kernels for 0% -> 0%
where the time goes in v2:
time: 302 us; the launch traced here: 296 us
  starting transfers between devices  90.9 us (30%)
  local copies, waits for them, and re-layouts  82.2 us (27%)
  waiting for transfers between devices  59.5 us (20%)
  Pallas kernels  29 us (10%)
  matrix products  16.7 us (6%)
  other arithmetic  16.6 us (5%)
    ppermute x8, starting transfers between devices, exchange_sum(): values = kept + lax.ppermute(sent, axis, route)  41.7 us
    ppermute x8, starting transfers between devices, exchange_sum(): other = lax.ppermute(values, axis, route)  29.8 us
    pallas_call x1, Pallas kernels, patch_pass(): pl.pallas_call(patch_kernel, grid=(steps,), in_specs=[block((rows, channe...  29 us
    ppermute x1, waiting for transfers between devices, per_device(): lax.ppermute(target[:, :, :height - 1], 'rows', [(i + 1, i) for i in rang...  26.8 us
    ppermute x8, waiting for transfers between devices, exchange_sum(): values = kept + lax.ppermute(sent, axis, route)  21 us
    conv_general_dilated x1, matrix products, regress(): lax.conv_general_dilated(grid_rows[None], kernel, window_strides=(1, 1),...  15.6 us
    unnamed x61, local copies, waits for them, and re-layouts  12.9 us
    all_to_all x1, starting transfers between devices, per_device(): lax.all_to_all(outgoing, 'rows', split_axis=0, concat_axis=0, tiled=True)  12.1 us
  transfers between devices with their start and end apart: 20, of which 16 were waited for; matrix products, arithmetic and copies ran while one was open for 24% of the time, Pallas kernels for 0%

profile of v2, /device:TPU:1, one launch (start us, length us, event | category | flops | bytes accessed | tf_op | source)
XLA Modules:
  0.0 296.4 jit_solution(10706194258647821249)
XLA Ops:
  5.8 3.2 %broadcast_select_fusion = bf16[32,2,64,144]{3,2,1,0:T(8,128)(2,1)} fusion(bf16[32,2,64,144]{3,2,1,0:T(8,128)(2,1)} %bitcast.90, pred[32,2]{1,0:T(8,128)(4,1)S(1)} %copy.57), kind=kLoop, calls=%fused_computation.10 | loop fusion | flops 589824 | bytes 2359360 | tf_op jit(solution)/shard_map/jit(_take)/select_n | solution.py:419
  9.0 12.1 %all-to-all-start = ((bf16[32,2,64,144]{3,2,1,0:T(8,128)(2,1)}), bf16[32,2,64,144]{3,2,1,0:T(8,128)(2,1)}, u32[]{:S(2)}, u32[]{:S(2)}) async-start(bf16[32,2,64,144]{3,2,1,0:T(8,128)(2,1)} %broadcast_select_fusion), calls=%async_computation | async-start | bytes 4194304 | tf_op jit(solution)/shard_map/all_to_all | solution.py:421
  23.3 4.6 %collective-permute-start = (bf16[1,100,1,256]{3,1,2,0:T(8,128)(2,1)}, bf16[1,100,1,256]{3,1,2,0:T(8,128)(2,1)}, u32[]{:S(2)}, u32[]{:S(2)}) collective-permute-start(bf16[1,100,1,256]{3,1,2,0:T(8,128)(2,1)} %slice.87), channel_id=1, source_target_pairs={{0,4},{4,8},{8,12},{12,16},{16,20},{20,24},{24,28},{28,32},{32,36}... | collective-permute-start | bytes 153608 | tf_op jit(solution)/shard_map/ppermute | solution.py:423
  38.1 26.8 %collective-permute-done.2 = bf16[1,64,11,256]{3,1,2,0:T(8,128)(2,1)S(1)} collective-permute-done((bf16[1,64,11,256]{3,1,2,0:T(8,128)(2,1)S(1)}, bf16[1,64,11,256]{3,1,2,0:T(8,128)(2,1)S(1)}, u32[]{:S(2)}, u32[]{:S(2)}) %collective-permute-start.2) | collective-permute-done | bytes 360480 | tf_op jit(solution)/shard_map/ppermute | solution.py:426
  66.0 5.4 %copy.52 = bf16[1,100,25,256]{1,0,3,2:T(2,128)(2,1)} copy(bf16[1,100,25,256]{3,1,2,0:T(8,128)(2,1)S(1)} %pad_maximum_fusion.1) | data formatting | bytes 2560000 | tf_op jit(solution)/shard_map/concatenate | solution.py:427
  71.4 15.6 %fusion.21 = f32[1,23,256,128]{3,0,2,1:T(1,128)S(1)} fusion(bf16[1,100,25,256]{1,0,3,2:T(2,128)(2,1)} %copy.52, bf16[128,3,3,100]{0,3,2,1:T(8,128)(2,1)S(1)} %copy-done.10), kind=kOutput, calls=%fused_computation.112 | convolution fusion | flops 1353062400 | bytes 4525056 | tf_op jit(solution)/shard_map/conv_general_dilated | solution.py:84
  89.1 5.5 %copy.53 = bf16[2,64,23,256]{1,0,3,2:T(2,128)(2,1)} copy(bf16[2,64,23,256]{3,1,2,0:T(8,128)(2,1)S(1)} %pad_maximum_fusion) | data formatting | bytes 3014656 | tf_op jit(solution)/shard_map/stack | solution.py:432
  94.6 8.6 %gather_fusion = bf16[32,2,64,12,12]{2,1,4,3,0:T(2,128)(2,1)S(1)} fusion(bf16[2,64,23,256]{1,0,3,2:T(2,128)(2,1)} %copy.53, s32[32]{0:T(128)S(1)} %get-tuple-element.29), kind=kCustom, calls=%fused_computation | custom fusion | bytes 2359808 | tf_op jit(solution)/shard_map/vmap()/gather | solution.py:396
  103.3 5.4 %fusion.19 = (bf16[32,1,64,144]{2,1,3,0:T(2,128)(2,1)}, bf16[32,1,64,144]{2,1,3,0:T(2,128)(2,1)}) fusion(bf16[32,2,64,144]{2,1,3,0:T(2,128)(2,1)S(1)} %bitcast.85), kind=kLoop, calls=%fused_computation.110 | loop fusion | bytes 2359296 | tf_op jit(solution)/shard_map/slice | solution.py:438
  108.7 4.8 %copy.67 = bf16[32,1,64,144]{3,2,0,1:T(8,128)(2,1)S(1)} copy(bf16[32,1,64,144]{2,1,3,0:T(2,128)(2,1)} %get-tuple-element.25) | data formatting | bytes 1179648
  113.5 3.4 %copy.66 = bf16[32,1,64,144]{3,2,0,1:T(8,128)(2,1)} copy(bf16[32,1,64,144]{2,1,3,0:T(2,128)(2,1)S(1)} %copy-done.2) | data formatting | bytes 1179648
  116.9 3.1 %gather_fusion.2 = bf16[32,64,144]{2,1,0:T(8,128)(2,1)} fusion(bf16[64,64,144]{2,1,0:T(8,128)(2,1)} %bitcast.23, s32[1024]{0:T(1024)S(1)} %pad_clamp_fusion), kind=kCustom, calls=%fused_computation.2 | custom fusion | bytes 1179776 | tf_op jit(solution)/shard_map/jit(_take)/gather | solution.py:435
  120.1 2.4 subtract_bitcast_fusion
  124.2 3.8 %copy.59 = bf16[32,144,128]{2,1,0:T(8,128)(2,1)} copy(bf16[32,144,128]{1,2,0:T(8,128)(2,1)} %maximum_bitcast_fusion) | data formatting | bytes 2359296 | tf_op jit(solution)/shard_map/transpose | solution.py:311
  133.4 29.0 %shard_map.145 = (f32[4608,64]{1,0:T(8,128)}, f32[32,128]{1,0:T(8,128)}, f32[128,1152]{1,0:T(8,128)}, f32[128,1152]{1,0:T(8,128)}, f32[64,128]{1,0:T(8,128)}) custom-call(bf16[4608,128]{1,0:T(8,128)(2,1)} %bitcast.91, f32[4608,64]{1,0:T(8,128)} %bitcast.86, f32[4608,8]{1,0:T(8,128)} %bitcast.87, f32[4608,128]{1,0:T(8,128)} %bitcast.88, ...), custom_call_target="tpu_custom_call" | custom-call | tf_op jit(solution)/shard_map/pallas_call | solution.py:258
  163.9 2.3 multiply_reduce_fusion
  172.9 7.5 %collective-permute-done.4 = f32[77312]{0:T(1024)S(1)} collective-permute-done((f32[77312]{0:T(1024)S(1)}, f32[77312]{0:T(1024)S(1)}, u32[]{:S(2)}, u32[]{:S(2)}) %collective-permute-start.4) | collective-permute-done | bytes 309280 | tf_op jit(solution)/shard_map/ppermute | solution.py:367
  182.0 3.4 %collective-permute-done.5 = f32[38656]{0:T(1024)S(1)} collective-permute-done((f32[38656]{0:T(1024)S(1)}, f32[38656]{0:T(1024)S(1)}, u32[]{:S(2)}, u32[]{:S(2)}) %collective-permute-start.5) | collective-permute-done | bytes 154656 | tf_op jit(solution)/shard_map/ppermute | solution.py:367
  185.6 25.3 %collective-permute-start.6 = (f32[19328]{0:T(1024)S(1)}, f32[19328]{0:T(1024)S(1)}, u32[]{:S(2)}, u32[]{:S(2)}) collective-permute-start(f32[19328]{0:T(1024)S(1)} %dynamic_slice.68), channel_id=1, source_target_pairs={{0,8},{4,12},{8,0},{12,4},{16,24},{20,28},{24,16},{28,20},{32,40},... | collective-permute-start | bytes 231944 | tf_op jit(solution)/shard_map/ppermute | solution.py:367
  212.9 3.0 collective-permute-start.7
  220.6 2.9 collective-permute-start.9
  224.7 4.0 %collective-permute-start.10 = (f32[1208]{0:T(1024)S(1)}, f32[1208]{0:T(1024)S(1)}, u32[]{:S(2)}, u32[]{:S(2)}) collective-permute-start(f32[1208]{0:T(1024)S(1)} %dynamic_slice.76), channel_id=1, source_target_pairs={{0,64},{4,68},{8,72},{12,76},{16,80},{20,84},{24,88},{28,92},{32,9... | collective-permute-start | bytes 14504 | tf_op jit(solution)/shard_map/ppermute | solution.py:367
  228.7 2.4 collective-permute-done.10
  231.3 4.0 %collective-permute-start.11 = (f32[1208]{0:T(1024)S(1)}, f32[1208]{0:T(1024)S(1)}, u32[]{:S(2)}, u32[]{:S(2)}) collective-permute-start(f32[1208]{0:T(1024)S(1)} %get-tuple-element.17), channel_id=1, source_target_pairs={{0,64},{4,68},{8,72},{12,76},{16,80},{20,84},{24,88},{28,92},{32,9... | collective-permute-start | bytes 14504 | tf_op jit(solution)/shard_map/ppermute | solution.py:372
  235.3 2.5 collective-permute-done.11
  238.0 2.4 collective-permute-start.12
  245.2 3.0 %collective-permute-start.14 = (f32[9664]{0:T(1024)S(1)}, f32[9664]{0:T(1024)S(1)}, u32[]{:S(2)}, u32[]{:S(2)}) collective-permute-start(f32[9664]{0:T(1024)S(1)} %dynamic_update_slice.53), channel_id=1, source_target_pairs={{0,2},{1,3},{2,0},{3,1},{4,6},{5,7},{6,4},{7,5},{8,10},{9,11},{10,... | collective-permute-start | bytes 115976 | tf_op jit(solution)/shard_map/ppermute | solution.py:372
  250.1 3.2 %collective-permute-start.15 = (f32[19328]{0:T(1024)S(1)}, f32[19328]{0:T(1024)S(1)}, u32[]{:S(2)}, u32[]{:S(2)}) collective-permute-start(f32[19328]{0:T(1024)S(1)} %dynamic_update_slice.55), channel_id=1, source_target_pairs={{0,8},{4,12},{8,0},{12,4},{16,24},{20,28},{24,16},{28,20},{32,40},... | collective-permute-start | bytes 231944 | tf_op jit(solution)/shard_map/ppermute | solution.py:372
  263.8 4.0 %collective-permute-done.17 = f32[77312]{0:T(1024)S(1)} collective-permute-done((f32[77312]{0:T(1024)S(1)}, f32[77312]{0:T(1024)S(1)}, u32[]{:S(2)}, u32[]{:S(2)}) %collective-permute-start.17) | collective-permute-done | bytes 309280 | tf_op jit(solution)/shard_map/ppermute | solution.py:372
  269.9 13.3 %collective-permute-start.18 = (f32[154624]{0:T(1024)S(1)}, f32[154624]{0:T(1024)S(1)}, u32[]{:S(2)}, u32[]{:S(2)}) collective-permute-start(f32[154624]{0:T(1024)S(1)} %dynamic_update_slice.61), channel_id=1, source_target_pairs={{0,128},{128,0},{1,129},{129,1},{2,130},{130,2},{3,131},{131,3},{4... | collective-permute-start | bytes 1855496 | tf_op jit(solution)/shard_map/ppermute | solution.py:372
  284.0 4.1 %dynamic_update_slice.62 = f32[309248]{0:T(1024)S(1)} dynamic-update-slice(f32[309248]{0:T(1024)S(1)} %broadcast_in_dim.43, f32[154624]{0:T(1024)S(1)} %dynamic_update_slice.61, s32[]{:T(128)S(6)} %select_n.385) | dynamic-update-slice | bytes 1236996 | tf_op jit(solution)/shard_map/dynamic_update_slice | solution.py:375
  288.2 4.2 %dynamic_update_slice.63 = f32[309248]{0:T(1024)S(1)} dynamic-update-slice(f32[309248]{0:T(1024)S(1)} %dynamic_update_slice.62, f32[154624]{0:T(1024)S(1)} %collective-permute-done.18, s32[]{:T(128)S(6)} %select_n.386) | dynamic-update-slice | bytes 1236996 | tf_op jit(solution)/shard_map/dynamic_update_slice | solution.py:376
  (193 shorter events, 69.6 us)
Async XLA Ops:
  9.0 12.1 %copy-start.7 = (bf16[1,100,12,256]{3,1,2,0:T(8,128)(2,1)S(1)}, bf16[1,100,12,256]{3,1,2,0:T(8,128)(2,1)}, u32[]{:S(2)}) copy-start(bf16[1,100,12,256]{3,1,2,0:T(8,128)(2,1)} %param.10) | copy-start | bytes 1843204
  9.0 18.8 %copy-start.5 = (bf16[1,64,12,256]{3,1,2,0:T(8,128)(2,1)S(1)}, bf16[1,64,12,256]{3,1,2,0:T(8,128)(2,1)}, u32[]{:S(2)}) copy-start(bf16[1,64,12,256]{3,1,2,0:T(8,128)(2,1)} %param.11) | copy-start | bytes 1179652
  9.0 22.6 %copy-start.11 = (bf16[128,900]{0,1:T(8,128)(2,1)S(1)}, bf16[128,900]{0,1:T(8,128)(2,1)}, u32[]{:S(2)}) copy-start(bf16[128,900]{0,1:T(8,128)(2,1)} %param.14) | copy-start | bytes 691204
  9.0 107.9 %all-to-all-start = ((bf16[32,2,64,144]{3,2,1,0:T(8,128)(2,1)}), bf16[32,2,64,144]{3,2,1,0:T(8,128)(2,1)}, u32[]{:S(2)}, u32[]{:S(2)}) async-start(bf16[32,2,64,144]{3,2,1,0:T(8,128)(2,1)} %broadcast_select_fusion), calls=%async_computation | async-start | bytes 4194304 | tf_op jit(solution)/shard_map/all_to_all | solution.py:421
  21.2 13.1 %copy-start.9 = (bf16[128,1152]{1,0:T(8,128)(2,1)S(1)}, bf16[128,1152]{1,0:T(8,128)(2,1)}, u32[]{:S(2)}) copy-start(bf16[128,1152]{1,0:T(8,128)(2,1)} %param.16) | copy-start | bytes 884740
  21.2 14.0 %copy-start.6 = (bf16[128,1152]{1,0:T(8,128)(2,1)S(1)}, bf16[128,1152]{1,0:T(8,128)(2,1)}, u32[]{:S(2)}) copy-start(bf16[128,1152]{1,0:T(8,128)(2,1)} %w2_ref.1) | copy-start | bytes 884740
  21.2 14.9 %copy-start.14 = (bf16[64,128]{1,0:T(8,128)(2,1)S(1)}, bf16[64,128]{1,0:T(8,128)(2,1)}, u32[]{:S(2)}) copy-start(bf16[64,128]{1,0:T(8,128)(2,1)} %pm_ref.1) | copy-start | bytes 49156
  21.2 15.6 %copy-start.18 = (f32[32,128]{1,0:T(8,128)S(1)}, f32[32,128]{1,0:T(8,128)}, u32[]{:S(2)}) copy-start(f32[32,128]{1,0:T(8,128)} %param.19) | copy-start | bytes 49156
  21.2 43.8 %collective-permute-start.1 = (bf16[1,100,12,256]{3,1,2,0:T(8,128)(2,1)S(1)}, bf16[1,100,12,256]{3,1,2,0:T(8,128)(2,1)S(1)}, u32[]{:S(2)}, u32[]{:S(2)}) collective-permute-start(bf16[1,100,12,256]{3,1,2,0:T(8,128)(2,1)S(1)} %copy-done.7), channel_id=1, source_target_pairs={{4,0},{8,4},{12,8},{16,12},{20,16},{24,20},{28,24},{32,28},{36,32}... | collective-permute-start | bytes 1843208 | tf_op jit(solution)/shard_map/ppermute | solution.py:424
  23.3 41.8 %collective-permute-start = (bf16[1,100,1,256]{3,1,2,0:T(8,128)(2,1)}, bf16[1,100,1,256]{3,1,2,0:T(8,128)(2,1)}, u32[]{:S(2)}, u32[]{:S(2)}) collective-permute-start(bf16[1,100,1,256]{3,1,2,0:T(8,128)(2,1)} %slice.87), channel_id=1, source_target_pairs={{0,4},{4,8},{8,12},{12,16},{16,20},{20,24},{24,28},{28,32},{32,36}... | collective-permute-start | bytes 153608 | tf_op jit(solution)/shard_map/ppermute | solution.py:423
  27.9 37.1 %collective-permute-start.2 = (bf16[1,64,11,256]{3,1,2,0:T(8,128)(2,1)S(1)}, bf16[1,64,11,256]{3,1,2,0:T(8,128)(2,1)S(1)}, u32[]{:S(2)}, u32[]{:S(2)}) collective-permute-start(bf16[1,64,11,256]{3,1,2,0:T(8,128)(2,1)S(1)} %slice.90), channel_id=1, source_target_pairs={{4,0},{8,4},{12,8},{16,12},{20,16},{24,20},{28,24},{32,28},{36,32}... | collective-permute-start | bytes 1081352 | tf_op jit(solution)/shard_map/ppermute | solution.py:426
  30.9 34.0 %copy-start.12 = (f32[32,32]{1,0:T(8,128)}, f32[32,32]{1,0:T(8,128)S(1)}, u32[]{:S(2)}) copy-start(f32[32,32]{1,0:T(8,128)S(1)} %fusion.5) | copy-start | bytes 12292
  71.4 15.6 %copy-start.24 = (bf16[64,128]{1,0:T(8,128)(2,1)S(1)}, bf16[64,128]{1,0:T(8,128)(2,1)}, u32[]{:S(2)}) copy-start(bf16[64,128]{1,0:T(8,128)(2,1)} %param.15) | copy-start | bytes 49156
  113.5 6.6 %copy-start.20 = (f32[32]{0:T(128)S(1)}, f32[32]{0:T(128)}, u32[]{:S(2)}) copy-start(f32[32]{0:T(128)} %get-tuple-element.33) | copy-start | bytes 388
  167.0 3.7 %collective-permute-start.3 = (f32[154624]{0:T(1024)S(1)}, f32[154624]{0:T(1024)S(1)}, u32[]{:S(2)}, u32[]{:S(2)}) collective-permute-start(f32[154624]{0:T(1024)S(1)} %pad_dynamic-slice_fusion), channel_id=1, source_target_pairs={{0,128},{128,0},{1,129},{129,1},{2,130},{130,2},{3,131},{131,3},{4... | collective-permute-start | bytes 1855496 | tf_op jit(solution)/shard_map/ppermute | solution.py:367
  170.9 9.4 %collective-permute-start.4 = (f32[77312]{0:T(1024)S(1)}, f32[77312]{0:T(1024)S(1)}, u32[]{:S(2)}, u32[]{:S(2)}) collective-permute-start(f32[77312]{0:T(1024)S(1)} %dynamic_slice.64), channel_id=1, source_target_pairs={{0,4},{4,0},{8,12},{12,8},{16,20},{20,16},{24,28},{28,24},{32,36},... | collective-permute-start | bytes 927752 | tf_op jit(solution)/shard_map/ppermute | solution.py:367
  180.6 4.8 %collective-permute-start.5 = (f32[38656]{0:T(1024)S(1)}, f32[38656]{0:T(1024)S(1)}, u32[]{:S(2)}, u32[]{:S(2)}) collective-permute-start(f32[38656]{0:T(1024)S(1)} %dynamic_slice.66), channel_id=1, source_target_pairs={{0,1},{1,0},{2,3},{3,2},{4,5},{5,4},{6,7},{7,6},{8,9},{9,8},{10,11... | collective-permute-start | bytes 463880 | tf_op jit(solution)/shard_map/ppermute | solution.py:367
  185.6 27.1 %collective-permute-start.6 = (f32[19328]{0:T(1024)S(1)}, f32[19328]{0:T(1024)S(1)}, u32[]{:S(2)}, u32[]{:S(2)}) collective-permute-start(f32[19328]{0:T(1024)S(1)} %dynamic_slice.68), channel_id=1, source_target_pairs={{0,8},{4,12},{8,0},{12,4},{16,24},{20,28},{24,16},{28,20},{32,40},... | collective-permute-start | bytes 231944 | tf_op jit(solution)/shard_map/ppermute | solution.py:367
  212.9 4.4 %collective-permute-start.7 = (f32[9664]{0:T(1024)S(1)}, f32[9664]{0:T(1024)S(1)}, u32[]{:S(2)}, u32[]{:S(2)}) collective-permute-start(f32[9664]{0:T(1024)S(1)} %dynamic_slice.70), channel_id=1, source_target_pairs={{0,2},{1,3},{2,0},{3,1},{4,6},{5,7},{6,4},{7,5},{8,10},{9,11},{10,... | collective-permute-start | bytes 115976 | tf_op jit(solution)/shard_map/ppermute | solution.py:367
  215.8 67.3 %copy-start.4 = (bf16[23,256,64]{1,2,0:T(8,128)(2,1)S(1)}, bf16[23,256,64]{1,2,0:T(8,128)(2,1)}, u32[]{:S(2)}) copy-start(bf16[23,256,64]{1,2,0:T(8,128)(2,1)} %copy-done.3) | copy-start | bytes 2260996
  217.4 3.0 collective-permute-start.8
  220.6 4.0 %collective-permute-start.9 = (f32[2416]{0:T(1024)S(1)}, f32[2416]{0:T(1024)S(1)}, u32[]{:S(2)}, u32[]{:S(2)}) collective-permute-start(f32[2416]{0:T(1024)S(1)} %dynamic_slice.74), channel_id=1, source_target_pairs={{0,32},{4,36},{8,40},{12,44},{16,48},{20,52},{24,56},{28,60},{32,0... | collective-permute-start | bytes 29000 | tf_op jit(solution)/shard_map/ppermute | solution.py:367
  224.7 6.4 %collective-permute-start.10 = (f32[1208]{0:T(1024)S(1)}, f32[1208]{0:T(1024)S(1)}, u32[]{:S(2)}, u32[]{:S(2)}) collective-permute-start(f32[1208]{0:T(1024)S(1)} %dynamic_slice.76), channel_id=1, source_target_pairs={{0,64},{4,68},{8,72},{12,76},{16,80},{20,84},{24,88},{28,92},{32,9... | collective-permute-start | bytes 14504 | tf_op jit(solution)/shard_map/ppermute | solution.py:367
  231.3 6.5 %collective-permute-start.11 = (f32[1208]{0:T(1024)S(1)}, f32[1208]{0:T(1024)S(1)}, u32[]{:S(2)}, u32[]{:S(2)}) collective-permute-start(f32[1208]{0:T(1024)S(1)} %get-tuple-element.17), channel_id=1, source_target_pairs={{0,64},{4,68},{8,72},{12,76},{16,80},{20,84},{24,88},{28,92},{32,9... | collective-permute-start | bytes 14504 | tf_op jit(solution)/shard_map/ppermute | solution.py:372
  238.0 3.5 %collective-permute-start.12 = (f32[2416]{0:T(1024)S(1)}, f32[2416]{0:T(1024)S(1)}, u32[]{:S(2)}, u32[]{:S(2)}) collective-permute-start(f32[2416]{0:T(1024)S(1)} %dynamic_update_slice.49), channel_id=1, source_target_pairs={{0,32},{4,36},{8,40},{12,44},{16,48},{20,52},{24,56},{28,60},{32,0... | collective-permute-start | bytes 29000 | tf_op jit(solution)/shard_map/ppermute | solution.py:372
  241.6 3.3 %collective-permute-start.13 = (f32[4832]{0:T(1024)S(1)}, f32[4832]{0:T(1024)S(1)}, u32[]{:S(2)}, u32[]{:S(2)}) collective-permute-start(f32[4832]{0:T(1024)S(1)} %dynamic_update_slice.51), channel_id=1, source_target_pairs={{0,16},{4,20},{8,24},{12,28},{16,0},{20,4},{24,8},{28,12},{32,48},... | collective-permute-start | bytes 57992 | tf_op jit(solution)/shard_map/ppermute | solution.py:372
  245.2 4.4 %collective-permute-start.14 = (f32[9664]{0:T(1024)S(1)}, f32[9664]{0:T(1024)S(1)}, u32[]{:S(2)}, u32[]{:S(2)}) collective-permute-start(f32[9664]{0:T(1024)S(1)} %dynamic_update_slice.53), channel_id=1, source_target_pairs={{0,2},{1,3},{2,0},{3,1},{4,6},{5,7},{6,4},{7,5},{8,10},{9,11},{10,... | collective-permute-start | bytes 115976 | tf_op jit(solution)/shard_map/ppermute | solution.py:372
  250.1 5.0 %collective-permute-start.15 = (f32[19328]{0:T(1024)S(1)}, f32[19328]{0:T(1024)S(1)}, u32[]{:S(2)}, u32[]{:S(2)}) collective-permute-start(f32[19328]{0:T(1024)S(1)} %dynamic_update_slice.55), channel_id=1, source_target_pairs={{0,8},{4,12},{8,0},{12,4},{16,24},{20,28},{24,16},{28,20},{32,40},... | collective-permute-start | bytes 231944 | tf_op jit(solution)/shard_map/ppermute | solution.py:372
  255.7 4.3 %collective-permute-start.16 = (f32[38656]{0:T(1024)S(1)}, f32[38656]{0:T(1024)S(1)}, u32[]{:S(2)}, u32[]{:S(2)}) collective-permute-start(f32[38656]{0:T(1024)S(1)} %dynamic_update_slice.57), channel_id=1, source_target_pairs={{0,1},{1,0},{2,3},{3,2},{4,5},{5,4},{6,7},{7,6},{8,9},{9,8},{10,11... | collective-permute-start | bytes 463880 | tf_op jit(solution)/shard_map/ppermute | solution.py:372
  261.2 6.7 %collective-permute-start.17 = (f32[77312]{0:T(1024)S(1)}, f32[77312]{0:T(1024)S(1)}, u32[]{:S(2)}, u32[]{:S(2)}) collective-permute-start(f32[77312]{0:T(1024)S(1)} %dynamic_update_slice.59), channel_id=1, source_target_pairs={{0,4},{4,0},{8,12},{12,8},{16,20},{20,16},{24,28},{28,24},{32,36},... | collective-permute-start | bytes 927752 | tf_op jit(solution)/shard_map/ppermute | solution.py:372
  269.9 18.3 %collective-permute-start.18 = (f32[154624]{0:T(1024)S(1)}, f32[154624]{0:T(1024)S(1)}, u32[]{:S(2)}, u32[]{:S(2)}) collective-permute-start(f32[154624]{0:T(1024)S(1)} %dynamic_update_slice.61), channel_id=1, source_target_pairs={{0,128},{128,0},{1,129},{129,1},{2,130},{130,2},{3,131},{131,3},{4... | collective-permute-start | bytes 1855496 | tf_op jit(solution)/shard_map/ppermute | solution.py:372
  288.1 8.1 %copy-start.1 = (bf16[1,1,64,64,144]{4,3,2,1,0:T(8,128)(2,1)S(1)}, bf16[1,1,64,64,144]{4,3,2,1,0:T(8,128)(2,1)}, u32[]{:S(2)}) copy-start(bf16[1,1,64,64,144]{4,3,2,1,0:T(8,128)(2,1)} %param.12) | copy-start | bytes 3538948
  (13 other events, 37.4 us)

commit v3 on v0

--- a/solution.py
+++ b/solution.py
@@ -421,9 +421,11 @@
     received = lax.all_to_all(outgoing, "rows", split_axis=0, concat_axis=0, tiled=True)
     count = strips
     above = lax.ppermute(coarse[:, :, -1:], "rows", [(i, i + 1) for i in range(count - 1)])
-    after = lax.ppermute(coarse, "rows", [(i + 1, i) for i in range(count - 1)])
     height = coarse.shape[2]
-    later = lax.ppermute(target[:, :, : height - 1], "rows", [(i + 1, i) for i in range(count - 1)])
+    both = jnp.concatenate([coarse, target], axis=1)
+    both = lax.ppermute(both, "rows", [(i + 1, i) for i in range(count - 1)])
+    after = both[:, : coarse.shape[1]]
+    later = both[:, coarse.shape[1] :, : height - 1]
     rimmed = jnp.concatenate([above, coarse, after], axis=2)
     mean_all = jnp.transpose(regress(rimmed[0], reg_conv, reg_out), (2, 0, 1))
     mean_strip = mean_all[:, :height]

time: 260 us -> 257 us (0.988)
  local copies, waits for them, and re-layouts: 72.4 us -> 68.5 us
  waiting for transfers between devices: 30.6 us -> 33.5 us
    ppermute x8, starting transfers between devices: 20.4 us -> 27 us  [exchange_sum(): values = kept + lax.ppermute(sent, axis, route)]
    ppermute x8, starting transfers between devices: 33.7 us -> 30.7 us  [exchange_sum(): other = lax.ppermute(values, axis, route)]
    ppermute x8, waiting for transfers between devices: 12.3 us -> 15.1 us  [exchange_sum(): other = lax.ppermute(values, axis, route)]
    unnamed x67 -> x51, local copies, waits for them, and re-layouts: 12.8 us -> 11.9 us
  transfers between devices with their start and end apart: 20 -> 19, of which waited for: 15 -> 15; matrix products, arithmetic and copies ran while one was open for 30% -> 28% of each run, Pallas kernels for 0% -> 0%
where the time goes in v3:
time: 257 us; the launch traced here: 253 us
  starting transfers between devices  76.9 us (30%)
  local copies, waits for them, and re-layouts  68.5 us (27%)
  waiting for transfers between devices  33.5 us (13%)
  Pallas kernels  28.8 us (11%)
  other arithmetic  23.1 us (9%)
  matrix products  17 us (7%)
  between operations  5.37 us (2%)
    ppermute x8, starting transfers between devices, exchange_sum(): other = lax.ppermute(values, axis, route)  30.7 us
    pallas_call x1, Pallas kernels, patch_pass(): pl.pallas_call(patch_kernel, grid=(steps,), in_specs=[block((rows, channe...  28.8 us
    ppermute x8, starting transfers between devices, exchange_sum(): values = kept + lax.ppermute(sent, axis, route)  27 us
    ppermute x8, waiting for transfers between devices, exchange_sum(): values = kept + lax.ppermute(sent, axis, route)  18.3 us
    conv_general_dilated x1, matrix products, regress(): lax.conv_general_dilated(grid_rows[None], kernel, window_strides=(1, 1),...  15.9 us
    ppermute x8, waiting for transfers between devices, exchange_sum(): other = lax.ppermute(values, axis, route)  15.1 us
    all_to_all x1, starting transfers between devices, per_device(): lax.all_to_all(outgoing, 'rows', split_axis=0, concat_axis=0, tiled=True)  13.4 us
    unnamed x51, local copies, waits for them, and re-layouts  11.9 us
  transfers between devices with their start and end apart: 19, of which 15 were waited for; matrix products, arithmetic and copies ran while one was open for 28% of the time, Pallas kernels for 0%

profile of v3, /device:TPU:1, one launch (start us, length us, event | category | flops | bytes accessed | tf_op | source)
XLA Modules:
  0.0 253.1 jit_solution(2919848128693082168)
XLA Ops:
  0.7 2.5 pad_maximum_fusion.2
  4.4 4.6 %collective-permute-start = (bf16[1,100,1,256]{3,1,2,0:T(8,128)(2,1)S(1)}, bf16[1,100,1,256]{3,1,2,0:T(8,128)(2,1)S(1)}, u32[]{:S(2)}, u32[]{:S(2)}) collective-permute-start(bf16[1,100,1,256]{3,1,2,0:T(8,128)(2,1)S(1)} %slice.115), channel_id=1, source_target_pairs={{0,4},{4,8},{8,12},{12,16},{16,20},{20,24},{24,28},{28,32},{32,36}... | collective-permute-start | bytes 153608 | tf_op jit(solution)/shard_map/ppermute | solution.py:423
  13.2 3.2 %broadcast_select_fusion = bf16[32,2,64,144]{3,2,1,0:T(8,128)(2,1)} fusion(bf16[32,2,64,144]{3,2,1,0:T(8,128)(2,1)} %bitcast.94, pred[32,2]{1,0:T(8,128)(4,1)S(1)} %copy.72), kind=kLoop, calls=%fused_computation.10 | loop fusion | flops 589824 | bytes 2359360 | tf_op jit(solution)/shard_map/jit(_take)/select_n | solution.py:419
  16.5 13.4 %all-to-all-start = ((bf16[32,2,64,144]{3,2,1,0:T(8,128)(2,1)}), bf16[32,2,64,144]{3,2,1,0:T(8,128)(2,1)}, u32[]{:S(2)}, u32[]{:S(2)}) async-start(bf16[32,2,64,144]{3,2,1,0:T(8,128)(2,1)} %broadcast_select_fusion), calls=%async_computation | async-start | bytes 4194304 | tf_op jit(solution)/shard_map/all_to_all | solution.py:421
  36.4 5.4 %copy.67 = bf16[1,100,25,256]{1,0,3,2:T(2,128)(2,1)} copy(bf16[1,100,25,256]{3,1,2,0:T(8,128)(2,1)S(1)} %pad_maximum_fusion.1) | data formatting | bytes 2560000 | tf_op jit(solution)/shard_map/concatenate | solution.py:429
  43.0 15.9 %fusion.20 = f32[1,23,256,128]{3,0,2,1:T(1,128)S(1)} fusion(bf16[1,100,25,256]{1,0,3,2:T(2,128)(2,1)} %copy.67, bf16[128,3,3,100]{0,3,2,1:T(8,128)(2,1)S(1)} %reshape.509), kind=kOutput, calls=%fused_computation.138 | convolution fusion | flops 1353062400 | bytes 4525056 | tf_op jit(solution)/shard_map/conv_general_dilated | solution.py:84
  61.1 5.4 %copy.68 = bf16[2,64,23,256]{1,0,3,2:T(2,128)(2,1)} copy(bf16[2,64,23,256]{3,1,2,0:T(8,128)(2,1)S(1)} %pad_maximum_fusion) | data formatting | bytes 3014656 | tf_op jit(solution)/shard_map/stack | solution.py:434
  66.5 8.6 %gather_fusion = bf16[32,2,64,12,12]{2,1,4,3,0:T(2,128)(2,1)S(1)} fusion(bf16[2,64,23,256]{1,0,3,2:T(2,128)(2,1)} %copy.68, s32[32]{0:T(128)S(1)} %get-tuple-element.43), kind=kCustom, calls=%fused_computation | custom fusion | bytes 2359808 | tf_op jit(solution)/shard_map/vmap()/gather | solution.py:396
  75.2 5.4 %fusion.18 = (bf16[32,1,64,144]{2,1,3,0:T(2,128)(2,1)}, bf16[32,1,64,144]{2,1,3,0:T(2,128)(2,1)}) fusion(bf16[32,2,64,144]{2,1,3,0:T(2,128)(2,1)S(1)} %bitcast.89), kind=kLoop, calls=%fused_computation.136 | loop fusion | bytes 2359296 | tf_op jit(solution)/shard_map/slice | solution.py:440
  80.6 4.8 %copy.93 = bf16[32,1,64,144]{3,2,0,1:T(8,128)(2,1)S(1)} copy(bf16[32,1,64,144]{2,1,3,0:T(2,128)(2,1)} %get-tuple-element.35) | data formatting | bytes 1179648
  85.4 3.4 %copy.92 = bf16[32,1,64,144]{3,2,0,1:T(8,128)(2,1)} copy(bf16[32,1,64,144]{2,1,3,0:T(2,128)(2,1)S(1)} %copy-done.2) | data formatting | bytes 1179648
  88.8 3.2 %gather_fusion.2 = bf16[32,64,144]{2,1,0:T(8,128)(2,1)} fusion(bf16[64,64,144]{2,1,0:T(8,128)(2,1)} %bitcast.23, s32[1024]{0:T(1024)S(1)} %pad_clamp_fusion), kind=kCustom, calls=%fused_computation.2 | custom fusion | bytes 1179776 | tf_op jit(solution)/shard_map/jit(_take)/gather | solution.py:437
  92.0 2.4 subtract_bitcast_fusion
  96.2 3.8 %copy.74 = bf16[32,144,128]{2,1,0:T(8,128)(2,1)} copy(bf16[32,144,128]{1,2,0:T(8,128)(2,1)} %maximum_bitcast_fusion) | data formatting | bytes 2359296 | tf_op jit(solution)/shard_map/transpose | solution.py:311
  99.9 2.1 copy.75
  105.2 28.8 %shard_map.145 = (f32[4608,64]{1,0:T(8,128)}, f32[32,128]{1,0:T(8,128)}, f32[128,1152]{1,0:T(8,128)}, f32[128,1152]{1,0:T(8,128)}, f32[64,128]{1,0:T(8,128)}) custom-call(bf16[4608,128]{1,0:T(8,128)(2,1)} %bitcast.96, f32[4608,64]{1,0:T(8,128)} %bitcast.90, f32[4608,8]{1,0:T(8,128)} %bitcast.91, f32[4608,128]{1,0:T(8,128)} %bitcast.92, ...), custom_call_target="tpu_custom_call" | custom-call | tf_op jit(solution)/shard_map/pallas_call | solution.py:258
  135.5 2.3 multiply_reduce_fusion
  144.7 7.1 %collective-permute-done.3 = f32[77312]{0:T(1024)S(1)} collective-permute-done((f32[77312]{0:T(1024)S(1)}, f32[77312]{0:T(1024)S(1)}, u32[]{:S(2)}, u32[]{:S(2)}) %collective-permute-start.3) | collective-permute-done | bytes 309280 | tf_op jit(solution)/shard_map/ppermute | solution.py:368
  153.2 2.8 %collective-permute-done.4 = f32[38656]{0:T(1024)S(1)} collective-permute-done((f32[38656]{0:T(1024)S(1)}, f32[38656]{0:T(1024)S(1)}, u32[]{:S(2)}, u32[]{:S(2)}) %collective-permute-start.4) | collective-permute-done | bytes 154656 | tf_op jit(solution)/shard_map/ppermute | solution.py:368
  156.1 3.0 %collective-permute-start.5 = (f32[19328]{0:T(1024)S(1)}, f32[19328]{0:T(1024)S(1)}, u32[]{:S(2)}, u32[]{:S(2)}) collective-permute-start(f32[19328]{0:T(1024)S(1)} %slice_select_fusion.2), channel_id=1, source_target_pairs={{0,8},{4,12},{8,0},{12,4},{16,24},{20,28},{24,16},{28,20},{32,40},... | collective-permute-start | bytes 231944 | tf_op jit(solution)/shard_map/ppermute | solution.py:368
  161.0 3.0 %collective-permute-start.6 = (f32[9664]{0:T(1024)S(1)}, f32[9664]{0:T(1024)S(1)}, u32[]{:S(2)}, u32[]{:S(2)}) collective-permute-start(f32[9664]{0:T(1024)S(1)} %slice_select_fusion.3), channel_id=1, source_target_pairs={{0,2},{1,3},{2,0},{3,1},{4,6},{5,7},{6,4},{7,5},{8,10},{9,11},{10,... | collective-permute-start | bytes 115976 | tf_op jit(solution)/shard_map/ppermute | solution.py:368
  168.5 4.9 %collective-permute-start.8 = (f32[2416]{0:T(1024)S(1)}, f32[2416]{0:T(1024)S(1)}, u32[]{:S(2)}, u32[]{:S(2)}) collective-permute-start(f32[2416]{0:T(1024)S(1)} %slice_select_fusion.5), channel_id=1, source_target_pairs={{0,32},{4,36},{8,40},{12,44},{16,48},{20,52},{24,56},{28,60},{32,0... | collective-permute-start | bytes 29000 | tf_op jit(solution)/shard_map/ppermute | solution.py:368
  174.6 10.1 %collective-permute-start.9 = (f32[1208]{0:T(1024)S(1)}, f32[1208]{0:T(1024)S(1)}, u32[]{:S(2)}, u32[]{:S(2)}) collective-permute-start(f32[1208]{0:T(1024)S(1)} %slice_select_fusion.6), channel_id=1, source_target_pairs={{0,64},{4,68},{8,72},{12,76},{16,80},{20,84},{24,88},{28,92},{32,9... | collective-permute-start | bytes 14504 | tf_op jit(solution)/shard_map/ppermute | solution.py:368
  185.9 5.5 %collective-permute-start.10 = (f32[1208]{0:T(1024)S(1)}, f32[1208]{0:T(1024)S(1)}, u32[]{:S(2)}, u32[]{:S(2)}) collective-permute-start(f32[1208]{0:T(1024)S(1)} %select_add_fusion.7), channel_id=1, source_target_pairs={{0,64},{4,68},{8,72},{12,76},{16,80},{20,84},{24,88},{28,92},{32,9... | collective-permute-start | bytes 14504 | tf_op jit(solution)/shard_map/ppermute | solution.py:373
  192.5 2.3 collective-permute-start.11
  196.1 2.9 %collective-permute-done.12 = f32[4832]{0:T(1024)S(1)} collective-permute-done((f32[4832]{0:T(1024)S(1)}, f32[4832]{0:T(1024)S(1)}, u32[]{:S(2)}, u32[]{:S(2)}) %collective-permute-start.12) | collective-permute-done | bytes 19360 | tf_op jit(solution)/shard_map/ppermute | solution.py:373
  199.1 3.0 %collective-permute-start.13 = (f32[9664]{0:T(1024)S(1)}, f32[9664]{0:T(1024)S(1)}, u32[]{:S(2)}, u32[]{:S(2)}) collective-permute-start(f32[9664]{0:T(1024)S(1)} %maximum_select_fusion.12), channel_id=1, source_target_pairs={{0,2},{1,3},{2,0},{3,1},{4,6},{5,7},{6,4},{7,5},{8,10},{9,11},{10,... | collective-permute-start | bytes 115976 | tf_op jit(solution)/shard_map/ppermute | solution.py:373
  203.6 3.1 %collective-permute-start.14 = (f32[19328]{0:T(1024)S(1)}, f32[19328]{0:T(1024)S(1)}, u32[]{:S(2)}, u32[]{:S(2)}) collective-permute-start(f32[19328]{0:T(1024)S(1)} %maximum_select_fusion.11), channel_id=1, source_target_pairs={{0,8},{4,12},{8,0},{12,4},{16,24},{20,28},{24,16},{28,20},{32,40},... | collective-permute-start | bytes 231944 | tf_op jit(solution)/shard_map/ppermute | solution.py:373
  210.3 2.7 %collective-permute-done.15 = f32[38656]{0:T(1024)S(1)} collective-permute-done((f32[38656]{0:T(1024)S(1)}, f32[38656]{0:T(1024)S(1)}, u32[]{:S(2)}, u32[]{:S(2)}) %collective-permute-start.15) | collective-permute-done | bytes 154656 | tf_op jit(solution)/shard_map/ppermute | solution.py:373
  213.7 5.1 %collective-permute-done.16 = f32[77312]{0:T(1024)S(1)} collective-permute-done((f32[77312]{0:T(1024)S(1)}, f32[77312]{0:T(1024)S(1)}, u32[]{:S(2)}, u32[]{:S(2)}) %collective-permute-start.16) | collective-permute-done | bytes 309280 | tf_op jit(solution)/shard_map/ppermute | solution.py:373
  219.0 15.3 %collective-permute-start.17 = (f32[154624]{0:T(1024)S(1)}, f32[154624]{0:T(1024)S(1)}, u32[]{:S(2)}, u32[]{:S(2)}) collective-permute-start(f32[154624]{0:T(1024)S(1)} %maximum_select_fusion.3), channel_id=1, source_target_pairs={{0,128},{128,0},{1,129},{129,1},{2,130},{130,2},{3,131},{131,3},{4... | collective-permute-start | bytes 1855496 | tf_op jit(solution)/shard_map/ppermute | solution.py:373
  244.2 2.3 reshape.524
  (187 shorter events, 59.2 us)
Async XLA Ops:
  0.6 10.6 %copy-start = (bf16[1,1,64,64,144]{4,3,2,1,0:T(8,128)(2,1)S(1)}, bf16[1,1,64,64,144]{4,3,2,1,0:T(8,128)(2,1)}, u32[]{:S(2)}) copy-start(bf16[1,1,64,64,144]{4,3,2,1,0:T(8,128)(2,1)} %param.12) | copy-start | bytes 3538948
  0.7 8.4 %copy-start.14 = (s32[1,32,32,4]{2,3,1,0:T(4,128)S(1)}, s32[1,32,32,4]{2,3,1,0:T(4,128)}, u32[]{:S(2)}) copy-start(s32[1,32,32,4]{2,3,1,0:T(4,128)} %param.13) | copy-start | bytes 49156
  3.1 32.0 %collective-permute-start.1 = (bf16[1,164,12,256]{3,1,2,0:T(8,128)(2,1)}, bf16[1,164,12,256]{3,1,2,0:T(8,128)(2,1)}, u32[]{:S(2)}, u32[]{:S(2)}) collective-permute-start(bf16[1,164,12,256]{3,1,2,0:T(8,128)(2,1)} %pad_maximum_fusion.2), channel_id=1, source_target_pairs={{4,0},{8,4},{12,8},{16,12},{20,16},{24,20},{28,24},{32,28},{36,32}... | collective-permute-start | bytes 3022856 | tf_op jit(solution)/shard_map/ppermute | solution.py:426
  4.4 31.8 %collective-permute-start = (bf16[1,100,1,256]{3,1,2,0:T(8,128)(2,1)S(1)}, bf16[1,100,1,256]{3,1,2,0:T(8,128)(2,1)S(1)}, u32[]{:S(2)}, u32[]{:S(2)}) collective-permute-start(bf16[1,100,1,256]{3,1,2,0:T(8,128)(2,1)S(1)} %slice.115), channel_id=1, source_target_pairs={{0,4},{4,8},{8,12},{12,16},{16,20},{20,24},{24,28},{28,32},{32,36}... | collective-permute-start | bytes 153608 | tf_op jit(solution)/shard_map/ppermute | solution.py:423
  16.5 14.2 %copy-start.17 = (f32[32,128]{1,0:T(8,128)S(1)}, f32[32,128]{1,0:T(8,128)}, u32[]{:S(2)}) copy-start(f32[32,128]{1,0:T(8,128)} %param.19) | copy-start | bytes 49156
  16.5 14.7 %copy-start.13 = (bf16[128,900]{0,1:T(8,128)(2,1)S(1)}, bf16[128,900]{0,1:T(8,128)(2,1)}, u32[]{:S(2)}) copy-start(bf16[128,900]{0,1:T(8,128)(2,1)} %param.14) | copy-start | bytes 691204
  16.5 16.1 %copy-start.12 = (bf16[128,1152]{1,0:T(8,128)(2,1)S(1)}, bf16[128,1152]{1,0:T(8,128)(2,1)}, u32[]{:S(2)}) copy-start(bf16[128,1152]{1,0:T(8,128)(2,1)} %param.16) | copy-start | bytes 884740
  16.5 72.3 %all-to-all-start = ((bf16[32,2,64,144]{3,2,1,0:T(8,128)(2,1)}), bf16[32,2,64,144]{3,2,1,0:T(8,128)(2,1)}, u32[]{:S(2)}, u32[]{:S(2)}) async-start(bf16[32,2,64,144]{3,2,1,0:T(8,128)(2,1)} %broadcast_select_fusion), calls=%async_computation | async-start | bytes 4194304 | tf_op jit(solution)/shard_map/all_to_all | solution.py:421
  36.4 6.6 %copy-start.9 = (bf16[1,64,12,256]{3,1,2,0:T(8,128)(2,1)S(1)}, bf16[1,64,12,256]{3,1,2,0:T(8,128)(2,1)}, u32[]{:S(2)}) copy-start(bf16[1,64,12,256]{3,1,2,0:T(8,128)(2,1)} %param.11) | copy-start | bytes 1179652
  43.0 16.0 %copy-start.19 = (bf16[64,128]{1,0:T(8,128)(2,1)S(1)}, bf16[64,128]{1,0:T(8,128)(2,1)}, u32[]{:S(2)}) copy-start(bf16[64,128]{1,0:T(8,128)(2,1)} %param.15) | copy-start | bytes 49156
  80.6 4.8 %copy-start.2 = (bf16[32,1,64,144]{2,1,3,0:T(2,128)(2,1)S(1)}, bf16[32,1,64,144]{2,1,3,0:T(2,128)(2,1)}, u32[]{:S(2)}) copy-start(bf16[32,1,64,144]{2,1,3,0:T(2,128)(2,1)} %get-tuple-element.34) | copy-start | bytes 1769476
  138.5 3.4 %collective-permute-start.2 = (f32[154624]{0:T(1024)S(1)}, f32[154624]{0:T(1024)}, u32[]{:S(2)}, u32[]{:S(2)}) collective-permute-start(f32[154624]{0:T(1024)S(1)} %fusion.2), channel_id=1, source_target_pairs={{0,128},{128,0},{1,129},{129,1},{2,130},{130,2},{3,131},{131,3},{4... | collective-permute-start | bytes 1855496 | tf_op jit(solution)/shard_map/ppermute | solution.py:368
  143.1 63.6 %copy-start.8 = (bf16[23,256,64]{1,2,0:T(8,128)(2,1)S(1)}, bf16[23,256,64]{1,2,0:T(8,128)(2,1)}, u32[]{:S(2)}) copy-start(bf16[23,256,64]{1,2,0:T(8,128)(2,1)} %copy-done.7) | copy-start | bytes 2260996
  143.1 8.7 %collective-permute-start.3 = (f32[77312]{0:T(1024)S(1)}, f32[77312]{0:T(1024)S(1)}, u32[]{:S(2)}, u32[]{:S(2)}) collective-permute-start(f32[77312]{0:T(1024)S(1)} %slice_select_fusion), channel_id=1, source_target_pairs={{0,4},{4,0},{8,12},{12,8},{16,20},{20,16},{24,28},{28,24},{32,36},... | collective-permute-start | bytes 927752 | tf_op jit(solution)/shard_map/ppermute | solution.py:368
  151.9 4.2 %collective-permute-start.4 = (f32[38656]{0:T(1024)S(1)}, f32[38656]{0:T(1024)S(1)}, u32[]{:S(2)}, u32[]{:S(2)}) collective-permute-start(f32[38656]{0:T(1024)S(1)} %slice_select_fusion.1), channel_id=1, source_target_pairs={{0,1},{1,0},{2,3},{3,2},{4,5},{5,4},{6,7},{7,6},{8,9},{9,8},{10,11... | collective-permute-start | bytes 463880 | tf_op jit(solution)/shard_map/ppermute | solution.py:368
  156.1 4.8 %collective-permute-start.5 = (f32[19328]{0:T(1024)S(1)}, f32[19328]{0:T(1024)S(1)}, u32[]{:S(2)}, u32[]{:S(2)}) collective-permute-start(f32[19328]{0:T(1024)S(1)} %slice_select_fusion.2), channel_id=1, source_target_pairs={{0,8},{4,12},{8,0},{12,4},{16,24},{20,28},{24,16},{28,20},{32,40},... | collective-permute-start | bytes 231944 | tf_op jit(solution)/shard_map/ppermute | solution.py:368
  161.0 4.4 %collective-permute-start.6 = (f32[9664]{0:T(1024)S(1)}, f32[9664]{0:T(1024)S(1)}, u32[]{:S(2)}, u32[]{:S(2)}) collective-permute-start(f32[9664]{0:T(1024)S(1)} %slice_select_fusion.3), channel_id=1, source_target_pairs={{0,2},{1,3},{2,0},{3,1},{4,6},{5,7},{6,4},{7,5},{8,10},{9,11},{10,... | collective-permute-start | bytes 115976 | tf_op jit(solution)/shard_map/ppermute | solution.py:368
  165.6 2.7 %collective-permute-start.7 = (f32[4832]{0:T(1024)S(1)}, f32[4832]{0:T(1024)S(1)}, u32[]{:S(2)}, u32[]{:S(2)}) collective-permute-start(f32[4832]{0:T(1024)S(1)} %slice_select_fusion.4), channel_id=1, source_target_pairs={{0,16},{4,20},{8,24},{12,28},{16,0},{20,4},{24,8},{28,12},{32,48},... | collective-permute-start | bytes 57992 | tf_op jit(solution)/shard_map/ppermute | solution.py:368
  168.5 6.0 %collective-permute-start.8 = (f32[2416]{0:T(1024)S(1)}, f32[2416]{0:T(1024)S(1)}, u32[]{:S(2)}, u32[]{:S(2)}) collective-permute-start(f32[2416]{0:T(1024)S(1)} %slice_select_fusion.5), channel_id=1, source_target_pairs={{0,32},{4,36},{8,40},{12,44},{16,48},{20,52},{24,56},{28,60},{32,0... | collective-permute-start | bytes 29000 | tf_op jit(solution)/shard_map/ppermute | solution.py:368
  174.6 11.2 %collective-permute-start.9 = (f32[1208]{0:T(1024)S(1)}, f32[1208]{0:T(1024)S(1)}, u32[]{:S(2)}, u32[]{:S(2)}) collective-permute-start(f32[1208]{0:T(1024)S(1)} %slice_select_fusion.6), channel_id=1, source_target_pairs={{0,64},{4,68},{8,72},{12,76},{16,80},{20,84},{24,88},{28,92},{32,9... | collective-permute-start | bytes 14504 | tf_op jit(solution)/shard_map/ppermute | solution.py:368
  185.9 6.5 %collective-permute-start.10 = (f32[1208]{0:T(1024)S(1)}, f32[1208]{0:T(1024)S(1)}, u32[]{:S(2)}, u32[]{:S(2)}) collective-permute-start(f32[1208]{0:T(1024)S(1)} %select_add_fusion.7), channel_id=1, source_target_pairs={{0,64},{4,68},{8,72},{12,76},{16,80},{20,84},{24,88},{28,92},{32,9... | collective-permute-start | bytes 14504 | tf_op jit(solution)/shard_map/ppermute | solution.py:373
  192.5 3.5 %collective-permute-start.11 = (f32[2416]{0:T(1024)S(1)}, f32[2416]{0:T(1024)S(1)}, u32[]{:S(2)}, u32[]{:S(2)}) collective-permute-start(f32[2416]{0:T(1024)S(1)} %maximum_select_fusion.14), channel_id=1, source_target_pairs={{0,32},{4,36},{8,40},{12,44},{16,48},{20,52},{24,56},{28,60},{32,0... | collective-permute-start | bytes 29000 | tf_op jit(solution)/shard_map/ppermute | solution.py:373
  196.0 3.0 %collective-permute-start.12 = (f32[4832]{0:T(1024)S(1)}, f32[4832]{0:T(1024)S(1)}, u32[]{:S(2)}, u32[]{:S(2)}) collective-permute-start(f32[4832]{0:T(1024)S(1)} %maximum_select_fusion.13), channel_id=1, source_target_pairs={{0,16},{4,20},{8,24},{12,28},{16,0},{20,4},{24,8},{28,12},{32,48},... | collective-permute-start | bytes 57992 | tf_op jit(solution)/shard_map/ppermute | solution.py:373
  199.1 4.4 %collective-permute-start.13 = (f32[9664]{0:T(1024)S(1)}, f32[9664]{0:T(1024)S(1)}, u32[]{:S(2)}, u32[]{:S(2)}) collective-permute-start(f32[9664]{0:T(1024)S(1)} %maximum_select_fusion.12), channel_id=1, source_target_pairs={{0,2},{1,3},{2,0},{3,1},{4,6},{5,7},{6,4},{7,5},{8,10},{9,11},{10,... | collective-permute-start | bytes 115976 | tf_op jit(solution)/shard_map/ppermute | solution.py:373
  203.6 4.9 %collective-permute-start.14 = (f32[19328]{0:T(1024)S(1)}, f32[19328]{0:T(1024)S(1)}, u32[]{:S(2)}, u32[]{:S(2)}) collective-permute-start(f32[19328]{0:T(1024)S(1)} %maximum_select_fusion.11), channel_id=1, source_target_pairs={{0,8},{4,12},{8,0},{12,4},{16,24},{20,28},{24,16},{28,20},{32,40},... | collective-permute-start | bytes 231944 | tf_op jit(solution)/shard_map/ppermute | solution.py:373
  208.5 4.5 %collective-permute-start.15 = (f32[38656]{0:T(1024)S(1)}, f32[38656]{0:T(1024)S(1)}, u32[]{:S(2)}, u32[]{:S(2)}) collective-permute-start(f32[38656]{0:T(1024)S(1)} %maximum_select_fusion.9), channel_id=1, source_target_pairs={{0,1},{1,0},{2,3},{3,2},{4,5},{5,4},{6,7},{7,6},{8,9},{9,8},{10,11... | collective-permute-start | bytes 463880 | tf_op jit(solution)/shard_map/ppermute | solution.py:373
  213.0 5.8 %collective-permute-start.16 = (f32[77312]{0:T(1024)S(1)}, f32[77312]{0:T(1024)S(1)}, u32[]{:S(2)}, u32[]{:S(2)}) collective-permute-start(f32[77312]{0:T(1024)S(1)} %maximum_select_fusion.5), channel_id=1, source_target_pairs={{0,4},{4,0},{8,12},{12,8},{16,20},{20,16},{24,28},{28,24},{32,36},... | collective-permute-start | bytes 927752 | tf_op jit(solution)/shard_map/ppermute | solution.py:373
  219.0 16.9 %copy-start.6 = (f32[154624]{0:T(1024)}, f32[154624]{0:T(1024)S(1)}, u32[]{:S(2)}) copy-start(f32[154624]{0:T(1024)S(1)} %maximum_select_fusion.3) | copy-start | bytes 1855492
  219.0 18.0 %collective-permute-start.17 = (f32[154624]{0:T(1024)S(1)}, f32[154624]{0:T(1024)S(1)}, u32[]{:S(2)}, u32[]{:S(2)}) collective-permute-start(f32[154624]{0:T(1024)S(1)} %maximum_select_fusion.3), channel_id=1, source_target_pairs={{0,128},{128,0},{1,129},{129,1},{2,130},{130,2},{3,131},{131,3},{4... | collective-permute-start | bytes 1855496 | tf_op jit(solution)/shard_map/ppermute | solution.py:373
  243.1 5.4 %copy-start.4 = (f32[4832,32]{0,1:T(8,128)S(1)}, f32[4832,32]{0,1:T(8,128)}, u32[]{:S(2)}) copy-start(f32[4832,32]{0,1:T(8,128)} %maximum_select_fusion.2) | copy-start | bytes 1855492
  243.1 5.4 %copy-start.5 = (f32[4832,32]{0,1:T(8,128)S(1)}, f32[4832,32]{0,1:T(8,128)}, u32[]{:S(2)}) copy-start(f32[4832,32]{0,1:T(8,128)} %copy.89) | copy-start | bytes 1855492
  243.1 8.7 %copy-start.1 = (bf16[1,1,64,64,144]{4,3,2,1,0:T(8,128)(2,1)S(1)}, bf16[1,1,64,64,144]{4,3,2,1,0:T(8,128)(2,1)}, u32[]{:S(2)}) copy-start(bf16[1,1,64,64,144]{4,3,2,1,0:T(8,128)(2,1)} %param.12) | copy-start | bytes 3538948
  (7 other events, 18.4 us)
